TPU v7x, 512 devices: a whole 4x4x16 slice. The times are simulated.
512 devices in a mesh: spec: 16 (over z_hi, y, core), neuron: 32 (over x, z_lo).
Axes of the slice: x: 4, y: 4, z: 16 (z_hi: 2, z_lo: 8; z = z_hi * 8 + z_lo), core: 2. Of those that a mesh axis runs over, the one named last changes fastest.
Arguments:
- class_scores: bfloat16 [384, 10, 32768], P('spec', None, 'neuron'), may hold values from -6 to 6
- true_class: int32 [384], P('spec'), may hold values from 0 to 9
- weight_blocks: bfloat16 [512, 64, 2048], P('neuron'), may hold values from -0.125 to 0.125
- col_blocks: int32 [512, 32], P('neuron'), may hold values from 0 to 511, as said below
- layer_bias: bfloat16 [32768], P('neuron'), may hold values from -0.119628906 to 0.119628906
- bound_mid: float32 [32768], P('neuron'), may hold values from -6 to 6
- bound_rad: float32 [32768], P('neuron'), may hold values from 0.05 to 2
- lower_slope: float32 [32768], P('neuron'), may hold values from 0 to 1
- unstable_blocks: int32 [512], P('neuron'), may hold values 0 or 1
Outputs:
- coefficients: bfloat16 [384, 9, 32768], P('spec', None, 'neuron')
- offsets: float32 [384, 9], P('spec')
Inputs may be any that keep to these rules, and one draw needn't show every extreme that they name: `col_blocks`: the 32 entries of a row r are distinct and name blocks of input neurons owned by the neuron index r // 16 or by its two neighbours on the closed loop of 32 indices.
All inputs are finite; a program needn't handle non-finite values. No bound on the sum of `unstable_blocks` on one device may be relied on, other than what follows from the above.
Results may differ from a plain program's by a relative error of at most 0.001.
The roundings to bfloat16 on the way count: a program that leaves them out, or rounds other values in their place, can miss the bound.
Values sent between devices are 32-bit elements; how exact they have to be, the bound alone decides.
No kernel may reach another device: no remote copies, remote signals or barrier semaphores. Data moves between devices by JAX's collectives and lax.ppermute only.
A program may use at most 64 MiB of HBM per device.

v0:
```python
import jax
import jax.numpy as jnp
from jax import lax
from jax.sharding import PartitionSpec as P


def from_behind(value, axis, by):
    length = lax.axis_size(axis)
    return lax.ppermute(value, axis, [(i, (i + by) % length) for i in range(length)])


def local(
    class_scores,
    true_class,
    weight_blocks,
    col_blocks,
    layer_bias,
    bound_mid,
    bound_rad,
    lower_slope,
    unstable_blocks,
):
    samples, classes, width = class_scores.shape
    specs = classes - 1
    rows = samples * specs
    per_dev = col_blocks.shape[0]
    blocksize = weight_blocks.shape[1]
    kept = col_blocks.shape[1]
    spec_ids = jnp.arange(specs, dtype=jnp.int32)
    others = spec_ids[None, :] + (spec_ids[None, :] >= true_class[:, None]).astype(jnp.int32)
    class_ids = jnp.arange(classes, dtype=jnp.int32)
    select = (true_class[:, None, None] == class_ids[None, None, :]).astype(jnp.float32) - (
        others[:, :, None] == class_ids[None, None, :]
    ).astype(jnp.float32)
    margin = jnp.einsum(
        "sjc,scn->sjn",
        select.astype(jnp.bfloat16),
        class_scores,
        preferred_element_type=jnp.float32,
    ).astype(jnp.bfloat16)
    margin_rows = margin.reshape(rows, width)
    position = lax.axis_index("neuron")
    total_blocks = per_dev * lax.axis_size("neuron")
    window = 3 * per_dev
    local_pos = (col_blocks - (position - 1) * per_dev) % total_blocks
    placing = (local_pos[:, :, None] == jnp.arange(window, dtype=jnp.int32)[None, None, :]).astype(
        jnp.bfloat16
    )
    blocks = weight_blocks.reshape(per_dev, blocksize, kept, blocksize)
    spread = jnp.einsum(
        "iakc,ikp->iapc", blocks, placing, preferred_element_type=jnp.float32
    ).astype(jnp.bfloat16)
    spread = spread.reshape(per_dev * blocksize, 3, width)
    joint = jnp.dot(
        margin_rows,
        spread.reshape(per_dev * blocksize, 3 * width),
        preferred_element_type=jnp.float32,
    )
    slots = joint.reshape(rows, 3, width)
    lower_part = slots[:, 0]
    upper_part = slots[:, 2]
    centre = slots[:, 1]
    from_higher = from_behind(lower_part, "neuron", -1)
    from_lower = from_behind(upper_part, "neuron", 1)
    bias_term = jnp.dot(margin_rows, layer_bias, preferred_element_type=jnp.float32)
    propagated = centre + from_higher + from_lower
    lower = bound_mid - bound_rad
    upper = bound_mid + bound_rad
    up_slope = (jax.nn.relu(upper) - jax.nn.relu(lower)) / (upper - lower)
    up_shift = jax.nn.relu(lower) - up_slope * lower
    flags = jnp.broadcast_to(unstable_blocks[:, None], (per_dev, blocksize)).reshape(width)
    low_slope = jnp.where(flags == 1, lower_slope, up_slope)
    negative = jnp.minimum(propagated, 0.0)
    coefficients = (low_slope * jnp.maximum(propagated, 0.0) + up_slope * negative).astype(
        jnp.bfloat16
    )
    shift_term = jnp.dot(negative, up_shift, precision=lax.Precision.HIGHEST)
    offsets = lax.psum(bias_term + shift_term, "neuron")
    return (coefficients.reshape(samples, specs, width), offsets.reshape(samples, specs))


def solution(mesh):
    placed = (
        P("spec", None, "neuron"),
        P("spec"),
        P("neuron", None, None),
        P("neuron", None),
        P("neuron"),
        P("neuron"),
        P("neuron"),
        P("neuron"),
        P("neuron"),
    )
    return jax.shard_map(
        local,
        mesh=mesh,
        in_specs=placed,
        out_specs=(P("spec", None, "neuron"), P("spec", None)),
        check_vma=False,
    )
```

profile of v0, /device:TPU:24, one launch (start us, length us, event | category | flops | bytes accessed | tf_op | source)
XLA Modules:
  0.0 349.7 jit_solution(14892758890128866745)
XLA Ops:
  0.6 0.0 copy-start
  0.6 0.8 convert_add_fusion
  1.4 0.7 fusion.11
  2.2 0.0 copy-done
  2.2 0.5 convolution_convert_fusion
  2.7 0.0 copy-start.1
  2.7 1.0 reshape.81
  3.7 0.0 copy-start.2
  3.7 12.8 %reshape.77 = bf16[16,64,32,64]{3,2,1,0:T(8,128)(2,1)} reshape(bf16[16,64,2048]{2,1,0:T(8,128)(2,1)} %param.11) | data formatting | bytes 8388608 | tf_op jit(solution)/shard_map/reshape | solution.py:49
  16.5 0.0 copy-done.1
  16.5 0.0 copy-done.2
  16.6 11.4 %convert_bitcast_fusion = bf16[16,64,48,64]{3,2,1,0:T(8,128)(2,1)} fusion(bf16[16,64,32,64]{3,2,1,0:T(8,128)(2,1)} %reshape.77, s32[16,32]{1,0:T(8,128)S(1)} %add_select_fusion), kind=kOutput, calls=%fused_computation | convolution fusion | flops 204496896 | bytes 10487808 | tf_op jit(solution)/shard_map/iakc,ikp->iapc/dot_general | solution.py:50
  28.0 16.3 %reshape_reshape.3 = bf16[1024,3072]{1,0:T(8,128)(2,1)} reshape(bf16[16,64,48,64]{3,2,1,0:T(8,128)(2,1)} %convert_bitcast_fusion) | data formatting | bytes 12582912 | tf_op jit(solution)/shard_map/reshape;reshape | solution.py:56
  44.3 8.6 %copy.15 = bf16[3072,1024]{1,0:T(8,128)(2,1)} copy(bf16[3072,1024]{0,1:T(8,128)(2,1)} %bitcast.36) | data formatting | bytes 12582912 | tf_op jit(solution)/shard_map/dot_general | solution.py:54
  52.9 0.0 copy-start.7
  52.9 0.0 copy-start.6
  52.9 0.0 copy-start.4
  52.9 0.0 copy-start.5
  52.9 0.0 copy-start.3
  52.9 5.0 %fusion.15 = f32[216,3,1024]{2,0,1:T(8,128)S(1)} fusion(bf16[216,1024,1]{1,0,2:T(8,128)(2,1)} %reshape.81, bf16[3,1024,1024]{2,1,0:T(8,128)(2,1)} %bitcast.35), kind=kOutput, calls=%fused_computation.31 | convolution fusion | flops 1358954496 | bytes 9388032 | tf_op jit(solution)/shard_map/dot_general | solution.py:54
  58.0 1.3 slice_bitcast_fusion.1
  59.3 15.3 %collective-permute-start = (f32[216,1024]{1,0:T(8,128)}, f32[216,1024]{1,0:T(8,128)}, u32[]{:S(2)}, u32[]{:S(2)}) collective-permute-start(f32[216,1024]{1,0:T(8,128)} %get-tuple-element.8), channel_id=1, source_target_pairs={{0,31},{1,0},{2,1},{3,2},{4,3},{5,4},{6,5},{7,6},{8,7},{9,8},{10,9... | collective-permute-start | bytes 2654216 | tf_op jit(solution)/shard_map/ppermute | solution.py:9
  74.7 1.9 collective-permute-start.1
  76.6 2.1 reshape.76
  78.7 0.0 copy-done.7
  78.7 0.1 broadcast_in_dim.2
  78.8 0.1 eq.58
  78.9 0.0 copy-done.6
  78.9 0.0 copy-done.4
  78.9 0.0 copy-done.5
  78.9 0.0 copy-done.3
  78.9 1.2 fusion.16
  80.2 14.8 %collective-permute-done = f32[216,1024]{1,0:T(8,128)} collective-permute-done((f32[216,1024]{1,0:T(8,128)}, f32[216,1024]{1,0:T(8,128)}, u32[]{:S(2)}, u32[]{:S(2)}) %collective-permute-start) | collective-permute-done | bytes 884768 | tf_op jit(solution)/shard_map/ppermute | solution.py:9
  95.0 18.6 %collective-permute-done.1 = f32[216,1024]{1,0:T(8,128)} collective-permute-done((f32[216,1024]{1,0:T(8,128)}, f32[216,1024]{1,0:T(8,128)}, u32[]{:S(2)}, u32[]{:S(2)}) %collective-permute-start.1) | collective-permute-done | bytes 884768 | tf_op jit(solution)/shard_map/ppermute | solution.py:9
  113.6 2.3 fusion.2
  115.9 0.1 reshape.79
  116.0 228.3 %psum.7 = f32[24,9]{1,0:T(8,128)S(1)} all-reduce(f32[24,9]{1,0:T(8,128)S(1)} %reshape.79), channel_id=1, replica_groups=mesh['spec'=16,'neuron'=32] {'neuron'}, use_global_device_ids=true, to_apply=%region_0.1 | all-reduce | flops 216 | bytes 1728 | tf_op jit(solution)/shard_map/psum | solution.py:78
  344.3 0.7 copy.17
  345.0 2.5 add_convert_fusion
  347.5 1.2 reshape.78
  348.6 1.0 copy.16
  (6 shorter events, 0.0 us)
Async XLA Ops:
  0.6 1.5 copy-start
  2.7 13.9 %copy-start.1 = (bf16[24,9,1024]{2,1,0:T(8,128)(2,1)}, bf16[24,9,1024]{2,1,0:T(8,128)(2,1)S(1)}, u32[]{:S(2)}) copy-start(bf16[24,9,1024]{2,1,0:T(8,128)(2,1)S(1)} %convolution_convert_fusion) | copy-start | bytes 1327108
  3.7 12.9 %copy-start.2 = (s32[16,32]{1,0:T(8,128)S(1)}, s32[16,32]{1,0:T(8,128)}, u32[]{:S(2)}) copy-start(s32[16,32]{1,0:T(8,128)} %param.12) | copy-start | bytes 6148
  52.9 25.8 %copy-start.7 = (s32[16]{0:T(128)S(1)}, s32[16]{0:T(128)}, u32[]{:S(2)}) copy-start(s32[16]{0:T(128)} %param.17) | copy-start | bytes 196
  52.9 25.9 %copy-start.6 = (bf16[1024]{0:T(1024)(128)(2,1)S(1)}, bf16[1024]{0:T(1024)(128)(2,1)}, u32[]{:S(2)}) copy-start(bf16[1024]{0:T(1024)(128)(2,1)} %param.13) | copy-start | bytes 6148
  52.9 26.0 %copy-start.4 = (f32[1024]{0:T(1024)S(1)}, f32[1024]{0:T(1024)}, u32[]{:S(2)}) copy-start(f32[1024]{0:T(1024)} %param.14) | copy-start | bytes 12292
  52.9 26.0 %copy-start.5 = (f32[1024]{0:T(1024)S(1)}, f32[1024]{0:T(1024)}, u32[]{:S(2)}) copy-start(f32[1024]{0:T(1024)} %param.15) | copy-start | bytes 12292
  52.9 26.0 %copy-start.3 = (f32[1024]{0:T(1024)S(1)}, f32[1024]{0:T(1024)}, u32[]{:S(2)}) copy-start(f32[1024]{0:T(1024)} %param.16) | copy-start | bytes 12292
  59.3 35.7 %collective-permute-start = (f32[216,1024]{1,0:T(8,128)}, f32[216,1024]{1,0:T(8,128)}, u32[]{:S(2)}, u32[]{:S(2)}) collective-permute-start(f32[216,1024]{1,0:T(8,128)} %get-tuple-element.8), channel_id=1, source_target_pairs={{0,31},{1,0},{2,1},{3,2},{4,3},{5,4},{6,5},{7,6},{8,7},{9,8},{10,9... | collective-permute-start | bytes 2654216 | tf_op jit(solution)/shard_map/ppermute | solution.py:9
  74.7 38.9 %collective-permute-start.1 = (f32[216,1024]{1,0:T(8,128)}, f32[216,1024]{1,0:T(8,128)}, u32[]{:S(2)}, u32[]{:S(2)}) collective-permute-start(f32[216,1024]{1,0:T(8,128)} %get-tuple-element.9), channel_id=1, source_target_pairs={{0,1},{1,2},{2,3},{3,4},{4,5},{5,6},{6,7},{7,8},{8,9},{9,10},{10,1... | collective-permute-start | bytes 2654216 | tf_op jit(solution)/shard_map/ppermute | solution.py:9
where the time goes:
time: 351 us; the launch traced here: 350 us
  blocking collectives  228 us (65%)
  local copies, waits for them, and re-layouts  45.4 us (13%)
  waiting for transfers between devices  33.4 us (10%)
  matrix products  20.5 us (6%)
  starting transfers between devices  17.2 us (5%)
  other arithmetic  4.04 us (1%)
    psum x1, blocking collectives, local(): offsets = lax.psum(bias_term + shift_term, 'neuron')  228 us
    ppermute x2, waiting for transfers between devices, from_behind(): lax.ppermute(value, axis, [(i, (i + by) % length) for i in range(length)])  33.4 us
    ppermute x2, starting transfers between devices, from_behind(): lax.ppermute(value, axis, [(i, (i + by) % length) for i in range(length)])  17.2 us
    another operation x1, local copies, waits for them, and re-layouts, local(): spread.reshape(per_dev * blocksize, 3 * width)  16.3 us
    reshape x1, local copies, waits for them, and re-layouts, local(): blocks = weight_blocks.reshape(per_dev, blocksize, kept, blocksize)  12.8 us
    dot_general x1, matrix products, local(): jnp.einsum('iakc,ikp->iapc', blocks, placing, preferred_element_type=jnp....  11.4 us
    dot_general x1, local copies, waits for them, and re-layouts, local(): jnp.dot(margin_rows, spread.reshape(per_dev * blocksize, 3 * width), pref...  8.62 us
  transfers between devices with their start and end apart: 2, of which 2 were waited for; matrix products, arithmetic and copies ran while one was open for 1% of the time, Pallas kernels for 0%

commit v1 on v0

v1 whole, which is shorter than its diff:
```python
import jax
import jax.numpy as jnp
from jax import lax
from jax.experimental import pallas as pl
from jax.experimental.pallas import tpu as pltpu
from jax.sharding import PartitionSpec as P

LANES = 128


def shift_by(value, axis, by):
    length = lax.axis_size(axis)
    return lax.ppermute(value, axis, [(i, (i + by) % length) for i in range(length)])


def products_kernel(
    base_ref,
    label_ref,
    cols_ref,
    scores_ref,
    bias_ref,
    weights_hbm,
    down_ref,
    centre_ref,
    up_ref,
    bias_acc_ref,
    tiles_ref,
    spread_ref,
    margin_ref,
    codes_ref,
    codes_smem,
    code_sem,
    sems,
):
    block_rows, blocksize, packed = weights_hbm.shape
    kept = packed // blocksize
    source_tiles = packed // LANES
    turned_at = source_tiles + 1
    classes, samples, width = scores_ref.shape
    specs = classes - 1
    chunks = sems.shape[0]
    per_chunk = block_rows // chunks
    copies = [
        pltpu.make_async_copy(
            weights_hbm.at[pl.ds(c * per_chunk, per_chunk)],
            tiles_ref.at[pl.ds(c * per_chunk, per_chunk), :, pl.ds(0, packed)],
            sems.at[c],
        )
        for c in range(chunks)
    ]
    for copy in copies:
        copy.start()

    total_blocks = lax.axis_size("neuron") * block_rows
    positions = (cols_ref[...] - base_ref[0]) & (total_blocks - 1)
    slot = lax.broadcasted_iota(jnp.int32, (block_rows, LANES), 1)
    found = jnp.full((block_rows, LANES), -1, jnp.int32)
    for k in range(kept):
        found = jnp.where(slot == positions[:, k : k + 1], k, found)
    same_half = (found & 1) == (slot & 1)
    tile = found >> 1
    codes = jnp.where(found < 0, source_tiles, jnp.where(same_half, tile, tile + turned_at))
    codes_ref[...] = codes
    code_copy = pltpu.make_async_copy(codes_ref, codes_smem, code_sem)
    code_copy.start()

    row = lax.broadcasted_iota(jnp.int32, (samples, width), 0)
    labels = jnp.zeros((samples, width), jnp.int32)
    for s in range(samples):
        labels = jnp.where(row == s, label_ref[s], labels)
    scores = [scores_ref[c].astype(jnp.float32) for c in range(classes)]
    top = scores[0]
    for c in range(1, classes):
        top = jnp.where(labels == c, scores[c], top)
    bias = bias_ref[...].astype(jnp.float32)
    for j in range(specs):
        rest = jnp.where(labels > j, scores[j], scores[j + 1])
        margin = (top - rest).astype(jnp.bfloat16)
        margin_ref[pl.ds(j * samples, samples), :] = margin
        terms = margin.astype(jnp.float32) * bias
        acc = terms[:, :LANES]
        for t in range(1, width // LANES):
            acc = acc + terms[:, t * LANES : (t + 1) * LANES]
        bias_acc_ref[pl.ds(j * samples, samples), :] = acc

    tiles_ref[:, :, packed : packed + LANES] = jnp.zeros((block_rows, blocksize, LANES), jnp.bfloat16)
    low_half = lax.broadcasted_iota(jnp.int32, (blocksize, LANES), 1) < blocksize
    code_copy.wait()

    for c in range(chunks):
        copies[c].wait()

        def place(i, carry):
            r = c * per_chunk + i
            first = pl.multiple_of(r * blocksize, blocksize)
            for t in range(source_tiles):
                source = tiles_ref[r, :, t * LANES : (t + 1) * LANES]
                at = (turned_at + t) * LANES
                tiles_ref[r, :, at : at + LANES] = pltpu.roll(source, blocksize, 1)
            for q in range(3 * width // LANES):
                left = pl.multiple_of(codes_smem[r, 2 * q] * LANES, LANES)
                right = pl.multiple_of(codes_smem[r, 2 * q + 1] * LANES, LANES)
                spread_ref[pl.ds(first, blocksize), q * LANES : (q + 1) * LANES] = jnp.where(
                    low_half, tiles_ref[r, :, pl.ds(left, LANES)], tiles_ref[r, :, pl.ds(right, LANES)]
                )
            return carry

        lax.fori_loop(0, per_chunk, place, 0)

    step = 256
    for part, out in ((0, down_ref), (2, up_ref), (1, centre_ref)):
        for t in range(width // step):
            at = part * width + t * step
            out[:, t * step : (t + 1) * step] = jnp.dot(
                margin_ref[...], spread_ref[:, at : at + step], preferred_element_type=jnp.float32
            )


def products(base, labels, cols, scores, bias, weights):
    classes, samples, width = scores.shape
    rows = (classes - 1) * samples
    block_rows, blocksize, packed = weights.shape
    part = jax.ShapeDtypeStruct((rows, width), jnp.float32)
    smem = pl.BlockSpec(memory_space=pltpu.SMEM)
    vmem = pl.BlockSpec(memory_space=pltpu.VMEM)
    return pl.pallas_call(
        products_kernel,
        out_shape=(part, part, part, jax.ShapeDtypeStruct((rows, LANES), jnp.float32)),
        in_specs=[smem, smem, vmem, vmem, vmem, pl.BlockSpec(memory_space=pl.ANY)],
        out_specs=(vmem, vmem, vmem, vmem),
        scratch_shapes=[
            pltpu.VMEM((block_rows, blocksize, 2 * packed + LANES), jnp.bfloat16),
            pltpu.VMEM((block_rows * blocksize, 3 * width), jnp.bfloat16),
            pltpu.VMEM((rows, width), jnp.bfloat16),
            pltpu.VMEM((block_rows, LANES), jnp.int32),
            pltpu.SMEM((block_rows, LANES), jnp.int32),
            pltpu.SemaphoreType.DMA,
            pltpu.SemaphoreType.DMA((4,)),
        ],
        compiler_params=pltpu.CompilerParams(vmem_limit_bytes=40 << 20),
        name="products",
    )(base, labels, cols, scores, bias, weights)


def relax_kernel(
    flags_ref,
    mid_ref,
    rad_ref,
    slope_ref,
    bias_acc_ref,
    centre_ref,
    higher_ref,
    lower_ref,
    coef_ref,
    offs_ref,
    acc_ref,
):
    step = pl.program_id(0)
    per_step, samples, width = coef_ref.shape
    rows = per_step * samples
    blocksize = width // flags_ref.shape[0]
    lower = mid_ref[...] - rad_ref[...]
    upper = mid_ref[...] + rad_ref[...]
    up_slope = (jnp.maximum(upper, 0.0) - jnp.maximum(lower, 0.0)) / (upper - lower)
    up_shift = jnp.maximum(lower, 0.0) - up_slope * lower
    block = lax.broadcasted_iota(jnp.int32, (1, width), 1) // blocksize
    flags = jnp.zeros((1, width), jnp.int32)
    for b in range(flags_ref.shape[0]):
        flags = jnp.where(block == b, flags_ref[b], flags)
    low_slope = jnp.where(flags == 1, slope_ref[...], up_slope)
    propagated = centre_ref[...] + higher_ref[...] + lower_ref[...]
    negative = jnp.minimum(propagated, 0.0)
    coef = (low_slope * jnp.maximum(propagated, 0.0) + up_slope * negative).astype(jnp.bfloat16)
    for j in range(per_step):
        coef_ref[j] = coef[j * samples : (j + 1) * samples]
    terms = negative * up_shift
    acc = bias_acc_ref[...]
    for t in range(width // LANES):
        acc = acc + terms[:, t * LANES : (t + 1) * LANES]
    acc_ref[pl.ds(pl.multiple_of(step * rows, 8), rows), :] = acc

    @pl.when(step == pl.num_programs(0) - 1)
    def _():
        ones = jnp.ones((8, LANES), jnp.float32)
        sums = lax.dot_general(
            ones,
            acc_ref[...],
            (((1,), (1,)), ((), ())),
            precision=lax.Precision.HIGHEST,
            preferred_element_type=jnp.float32,
        )
        for d in range(offs_ref.shape[0]):
            offs_ref[d] = sums[:1]


def relax(flags, mid, rad, slope, bias_acc, centre, higher, lower, samples, devices):
    rows, width = centre.shape
    specs = rows // samples
    steps = 3
    per_step = specs // steps
    smem = pl.BlockSpec(memory_space=pltpu.SMEM)
    vector = pl.BlockSpec((1, width), lambda i: (0, 0))
    part = pl.BlockSpec((rows // steps, width), lambda i: (i, 0))
    return pl.pallas_call(
        relax_kernel,
        grid=(steps,),
        out_shape=(
            jax.ShapeDtypeStruct((specs, samples, width), jnp.bfloat16),
            jax.ShapeDtypeStruct((devices, 1, rows), jnp.float32),
        ),
        in_specs=[
            smem,
            vector,
            vector,
            vector,
            pl.BlockSpec((rows // steps, LANES), lambda i: (i, 0)),
            part,
            part,
            part,
        ],
        out_specs=(
            pl.BlockSpec((per_step, samples, width), lambda i: (i, 0, 0)),
            pl.BlockSpec((devices, 1, rows), lambda i: (0, 0, 0)),
        ),
        scratch_shapes=[pltpu.VMEM((rows, LANES), jnp.float32)],
        name="relax",
    )(flags, mid, rad, slope, bias_acc, centre, higher, lower)


def total_kernel(parts_ref, out_ref):
    specs, samples = out_ref.shape
    sums = parts_ref[0]
    for d in range(1, parts_ref.shape[0]):
        sums = sums + parts_ref[d]
    for j in range(specs):
        out_ref[j : j + 1, :] = sums[:, j * samples : (j + 1) * samples]


def local(
    class_scores,
    true_class,
    weight_blocks,
    col_blocks,
    layer_bias,
    bound_mid,
    bound_rad,
    lower_slope,
    unstable_blocks,
):
    samples, classes, width = class_scores.shape
    specs = classes - 1
    per_dev = col_blocks.shape[0]
    devices = lax.axis_size("neuron")
    base = ((lax.axis_index("neuron") - 1) * per_dev).astype(jnp.int32).reshape(1)
    down, centre, up, bias_acc = products(
        base,
        true_class,
        col_blocks,
        jnp.transpose(class_scores, (1, 0, 2)),
        layer_bias.reshape(1, width),
        weight_blocks,
    )
    higher = shift_by(down, "neuron", -1)
    lower = shift_by(up, "neuron", 1)
    coef, offs = relax(
        unstable_blocks,
        bound_mid.reshape(1, width),
        bound_rad.reshape(1, width),
        lower_slope.reshape(1, width),
        bias_acc,
        centre,
        higher,
        lower,
        samples,
        devices,
    )
    gathered = lax.all_to_all(offs, "neuron", 0, 0)
    offsets = pl.pallas_call(
        total_kernel,
        out_shape=jax.ShapeDtypeStruct((specs, samples), jnp.float32),
        name="total",
    )(gathered)
    return jnp.transpose(coef, (1, 0, 2)), offsets.T


def solution(mesh):
    placed = (
        P("spec", None, "neuron"),
        P("spec"),
        P("neuron", None, None),
        P("neuron", None),
        P("neuron"),
        P("neuron"),
        P("neuron"),
        P("neuron"),
        P("neuron"),
    )
    return jax.shard_map(
        local,
        mesh=mesh,
        in_specs=placed,
        out_specs=(P("spec", None, "neuron"), P("spec", None)),
        check_vma=False,
    )
```

time: 351 us -> 93.6 us (0.27)
  blocking collectives: 228 us -> 18.3 us
  local copies, waits for them, and re-layouts: 45.4 us -> 7.74 us
  matrix products: 20.5 us -> 0 us
  Pallas kernels: 0 us -> 12.6 us
  other arithmetic: 4.04 us -> 0 us
    psum x1 -> x0, blocking collectives: 228 us -> none  [local(): offsets = lax.psum(bias_term + shift_term, 'neuron')]
    dot_general x5 -> x0, matrix products: 20.5 us -> none  [the longest x1 11.4 us: local(): jnp.einsum('iakc,ikp->iapc', blocks, placing, preferred_element_type=jnp....]
    all_to_all x0 -> x1, blocking collectives: none -> 18.3 us  [local(): gathered = lax.all_to_all(offs, 'neuron', 0, 0)]
    reshape x5 -> x1, local copies, waits for them, and re-layouts: 17.2 us -> 0.69 us  [local(): layer_bias.reshape(1, width)]
    another operation x1 -> x0, local copies, waits for them, and re-layouts: 16.3 us -> none  [local(): spread.reshape(per_dev * blocksize, 3 * width)]
    pallas_call x0 -> x3, Pallas kernels: none -> 12.6 us  [the longest x1 7.42 us: products(): pl.pallas_call(products_kernel, out_shape=(part, part, part, jax.ShapeDty...]
    dot_general x1 -> x0, local copies, waits for them, and re-layouts: 8.62 us -> none  [local(): jnp.dot(margin_rows, spread.reshape(per_dev * blocksize, 3 * width), pref...]
    unnamed x19 -> x16, local copies, waits for them, and re-layouts: 1.75 us -> 7.06 us
  transfers between devices with their start and end apart: 2 -> 2, of which waited for: 2 -> 2; matrix products, arithmetic and copies ran while one was open for 1% -> 0% of each run, Pallas kernels for 0% -> 0%
where the time goes in v1:
time: 93.6 us; the launch traced here: 93.2 us
  waiting for transfers between devices  36.7 us (39%)
  blocking collectives  18.3 us (20%)
  starting transfers between devices  17.3 us (18%)
  Pallas kernels  12.6 us (13%)
  local copies, waits for them, and re-layouts  7.74 us (8%)
    ppermute x2, waiting for transfers between devices, shift_by(): lax.ppermute(value, axis, [(i, (i + by) % length) for i in range(length)])  36.7 us
    all_to_all x1, blocking collectives, local(): gathered = lax.all_to_all(offs, 'neuron', 0, 0)  18.3 us
    ppermute x2, starting transfers between devices, shift_by(): lax.ppermute(value, axis, [(i, (i + by) % length) for i in range(length)])  17.3 us
    pallas_call x1, Pallas kernels, products(): pl.pallas_call(products_kernel, out_shape=(part, part, part, jax.ShapeDty...  7.42 us
    unnamed x16, local copies, waits for them, and re-layouts  7.06 us
    pallas_call x1, Pallas kernels, relax(): pl.pallas_call(relax_kernel, grid=(steps,), out_shape=(jax.ShapeDtypeStru...  3.68 us
  transfers between devices with their start and end apart: 2, of which 2 were waited for; matrix products, arithmetic and copies ran while one was open for 0% of the time, Pallas kernels for 0%

profile of v1, /device:TPU:24, one launch (start us, length us, event | category | flops | bytes accessed | tf_op | source)
XLA Modules:
  0.0 93.2 jit_solution(17750205769318282402)
XLA Ops:
  0.6 0.7 reshape.23.bias_ref
  1.3 0.0 copy-start
  1.3 2.2 %copy-done = bf16[16,64,2048]{2,1,0:T(8,128)(2,1)S(1)} copy-done((bf16[16,64,2048]{2,1,0:T(8,128)(2,1)S(1)}, bf16[16,64,2048]{2,1,0:T(8,128)(2,1)}, u32[]{:S(2)}) %copy-start) | copy-done | bytes 4194328
  3.5 0.0 copy-start.2
  3.5 1.0 %copy-done.2 = bf16[24,10,1024]{2,0,1:T(8,128)(2,1)S(1)} copy-done((bf16[24,10,1024]{2,0,1:T(8,128)(2,1)S(1)}, bf16[24,10,1024]{2,0,1:T(8,128)(2,1)}, u32[]{:S(2)}) %copy-start.2) | copy-done | bytes 491544
  4.5 0.0 copy-start.4
  4.5 0.7 copy-done.4
  5.2 0.0 copy-start.5
  5.2 0.7 copy-done.5
  5.9 7.4 %products.1 = (f32[216,1024]{1,0:T(8,128)S(1)}, f32[216,1024]{1,0:T(8,128)S(1)}, f32[216,1024]{1,0:T(8,128)S(1)}, f32[216,128]{1,0:T(8,128)S(1)}) custom-call(s32[1]{0:T(128)} %bitcast.3.base_ref, s32[24]{0:T(128)S(1)} %copy-done.5, s32[16,32]{1,0:T(8,128)S(1)} %copy-done.4, bf16[10,24,1024]{2,1,0:T(8,128)(2,1)S(1)} %bitcast.7, ...), custom_call_target="tpu_custom_call" | custom-call | tf_op jit(solution)/shard_map/products/pallas_call | solution.py:126
  13.3 0.0 copy-start.1
  13.3 0.9 copy-done.1
  14.2 0.0 copy-start.3
  14.2 0.6 copy-done.3
  14.9 15.3 %collective-permute-start = (f32[216,1024]{1,0:T(8,128)S(1)}, f32[216,1024]{1,0:T(8,128)S(1)}, u32[]{:S(2)}, u32[]{:S(2)}) collective-permute-start(f32[216,1024]{1,0:T(8,128)S(1)} %get-tuple-element.10), channel_id=1, source_target_pairs={{0,31},{1,0},{2,1},{3,2},{4,3},{5,4},{6,5},{7,6},{8,7},{9,8},{10,9... | collective-permute-start | bytes 2654216 | tf_op jit(solution)/shard_map/ppermute | solution.py:13
  30.2 1.9 %collective-permute-start.1 = (f32[216,1024]{1,0:T(8,128)S(1)}, f32[216,1024]{1,0:T(8,128)S(1)}, u32[]{:S(2)}, u32[]{:S(2)}) collective-permute-start(f32[216,1024]{1,0:T(8,128)S(1)} %get-tuple-element.11), channel_id=1, source_target_pairs={{0,1},{1,2},{2,3},{3,4},{4,5},{5,6},{6,7},{7,8},{8,9},{9,10},{10,1... | collective-permute-start | bytes 2654216 | tf_op jit(solution)/shard_map/ppermute | solution.py:13
  32.1 18.1 %collective-permute-done.higher_ref = f32[216,1024]{1,0:T(8,128)S(1)} collective-permute-done((f32[216,1024]{1,0:T(8,128)S(1)}, f32[216,1024]{1,0:T(8,128)S(1)}, u32[]{:S(2)}, u32[]{:S(2)}) %collective-permute-start) | collective-permute-done | bytes 884768 | tf_op jit(solution)/shard_map/ppermute | solution.py:13
  50.2 0.0 copy-start.6
  50.2 18.6 %collective-permute-done.1.lower_ref = f32[216,1024]{1,0:T(8,128)S(1)} collective-permute-done((f32[216,1024]{1,0:T(8,128)S(1)}, f32[216,1024]{1,0:T(8,128)S(1)}, u32[]{:S(2)}, u32[]{:S(2)}) %collective-permute-start.1) | collective-permute-done | bytes 884768 | tf_op jit(solution)/shard_map/ppermute | solution.py:13
  68.8 0.0 copy-start.7
  68.8 0.0 copy-done.6
  68.8 0.9 %copy-done.7 = f32[216,1024]{1,0:T(8,128)} copy-done((f32[216,1024]{1,0:T(8,128)}, f32[216,1024]{1,0:T(8,128)S(1)}, u32[]{:S(2)}) %copy-start.7) | copy-done | bytes 884760
  69.8 3.7 %relax.1 = (bf16[9,24,1024]{2,1,0:T(8,128)(2,1)}, f32[32,1,216]{2,1,0:T(1,128)}) custom-call(s32[16]{0:T(128)} %flags_ref.1, f32[1,1024]{1,0:T(1,128)} %bitcast.9, f32[1,1024]{1,0:T(1,128)} %bitcast.10, f32[1,1024]{1,0:T(1,128)} %bitcast.11, f32[216,128]{1,0:T(8,128)} %copy-done.3, f32[216,1024]{1,0:T(8,128)} %copy-done.1, f32[216,1024]{1,0:T(8,128)} %copy-done.6, ...), custom_call_target="tpu_custom_call" | custom-call | tf_op jit(solution)/shard_map/relax/pallas_call | solution.py:204
  73.4 18.3 %all_to_all.5.parts_ref = f32[32,1,216]{2,1,0:T(1,128)} all-to-all(f32[32,1,216]{2,1,0:T(1,128)} %get-tuple-element.13), channel_id=1, replica_groups=mesh['spec'=16,'neuron'=32] {'neuron'}, dimensions={0} | all-to-all | bytes 55296 | tf_op jit(solution)/shard_map/all_to_all | solution.py:277
  91.7 1.5 %total.1 = f32[9,24]{1,0:T(8,128)} custom-call(f32[32,1,216]{2,1,0:T(1,128)} %all_to_all.5.parts_ref), custom_call_target="tpu_custom_call" | custom-call | tf_op jit(solution)/shard_map/total/pallas_call | solution.py:278
Async XLA Ops:
  1.3 2.2 %copy-start = (bf16[16,64,2048]{2,1,0:T(8,128)(2,1)S(1)}, bf16[16,64,2048]{2,1,0:T(8,128)(2,1)}, u32[]{:S(2)}) copy-start(bf16[16,64,2048]{2,1,0:T(8,128)(2,1)} %weights_hbm.1) | copy-start | bytes 12582916
  3.5 1.0 %copy-start.2 = (bf16[24,10,1024]{2,0,1:T(8,128)(2,1)S(1)}, bf16[24,10,1024]{2,0,1:T(8,128)(2,1)}, u32[]{:S(2)}) copy-start(bf16[24,10,1024]{2,0,1:T(8,128)(2,1)} %param.9) | copy-start | bytes 1474564
  4.5 0.7 copy-start.4
  5.2 0.7 copy-start.5
  13.3 0.9 copy-start.1
  14.2 0.6 copy-start.3
  14.9 35.4 %collective-permute-start = (f32[216,1024]{1,0:T(8,128)S(1)}, f32[216,1024]{1,0:T(8,128)S(1)}, u32[]{:S(2)}, u32[]{:S(2)}) collective-permute-start(f32[216,1024]{1,0:T(8,128)S(1)} %get-tuple-element.10), channel_id=1, source_target_pairs={{0,31},{1,0},{2,1},{3,2},{4,3},{5,4},{6,5},{7,6},{8,7},{9,8},{10,9... | collective-permute-start | bytes 2654216 | tf_op jit(solution)/shard_map/ppermute | solution.py:13
  30.2 38.6 %collective-permute-start.1 = (f32[216,1024]{1,0:T(8,128)S(1)}, f32[216,1024]{1,0:T(8,128)S(1)}, u32[]{:S(2)}, u32[]{:S(2)}) collective-permute-start(f32[216,1024]{1,0:T(8,128)S(1)} %get-tuple-element.11), channel_id=1, source_target_pairs={{0,1},{1,2},{2,3},{3,4},{4,5},{5,6},{6,7},{7,8},{8,9},{9,10},{10,1... | collective-permute-start | bytes 2654216 | tf_op jit(solution)/shard_map/ppermute | solution.py:13
  50.2 18.6 %copy-start.6 = (f32[216,1024]{1,0:T(8,128)}, f32[216,1024]{1,0:T(8,128)S(1)}, u32[]{:S(2)}) copy-start(f32[216,1024]{1,0:T(8,128)S(1)} %collective-permute-done.higher_ref) | copy-start | bytes 2654212
  68.8 0.9 %copy-start.7 = (f32[216,1024]{1,0:T(8,128)}, f32[216,1024]{1,0:T(8,128)S(1)}, u32[]{:S(2)}) copy-start(f32[216,1024]{1,0:T(8,128)S(1)} %collective-permute-done.1.lower_ref) | copy-start | bytes 2654212

commit v2 on v1

v2 whole, which is shorter than its diff:
```python
import functools

import jax
import jax.numpy as jnp
from jax import lax
from jax.experimental import pallas as pl
from jax.experimental.pallas import tpu as pltpu
from jax.sharding import PartitionSpec as P

LANES = 128
CHUNKS = 4


def shift_by(value, axis, by):
    length = lax.axis_size(axis)
    return lax.ppermute(value, axis, [(i, (i + by) % length) for i in range(length)])


def start_weights(weights_hbm, tiles_ref, sems):
    packed = weights_hbm.shape[2]
    per_chunk = weights_hbm.shape[0] // CHUNKS
    copies = [
        pltpu.make_async_copy(
            weights_hbm.at[pl.ds(c * per_chunk, per_chunk)],
            tiles_ref.at[pl.ds(c * per_chunk, per_chunk), :, pl.ds(0, packed)],
            sems.at[c],
        )
        for c in range(CHUNKS)
    ]
    for copy in copies:
        copy.start()
    return copies


def make_codes(cols, base, total_blocks, source_tiles):
    block_rows, kept = cols.shape
    positions = (cols - base) & (total_blocks - 1)
    slot = lax.broadcasted_iota(jnp.int32, (block_rows, LANES), 1)
    found = jnp.full((block_rows, LANES), -1, jnp.int32)
    for k in range(kept):
        found = jnp.where(slot == positions[:, k : k + 1], k, found)
    same_half = (found & 1) == (slot & 1)
    tile = found >> 1
    return jnp.where(found < 0, source_tiles, jnp.where(same_half, tile, tile + source_tiles + 1))


def place_and_multiply(tiles_ref, spread_ref, codes_smem, margin_ref, copies, parts, outs):
    block_rows, blocksize, lanes = tiles_ref.shape
    source_tiles = (lanes // LANES - 1) // 2
    turned_at = source_tiles + 1
    per_chunk = block_rows // CHUNKS
    width = margin_ref.shape[1]
    empty = slice(source_tiles * LANES, turned_at * LANES)
    tiles_ref[:, :, empty] = jnp.zeros((block_rows, blocksize, LANES), jnp.bfloat16)
    low_half = lax.broadcasted_iota(jnp.int32, (blocksize, LANES), 1) < blocksize
    per_part = width // LANES
    for c in range(CHUNKS):
        copies[c].wait()

        def place(i, carry):
            r = c * per_chunk + i
            first = pl.multiple_of(r * blocksize, blocksize)
            for t in range(source_tiles):
                at = (turned_at + t) * LANES
                tiles_ref[r, :, at : at + LANES] = pltpu.roll(
                    tiles_ref[r, :, t * LANES : (t + 1) * LANES], blocksize, 1
                )
            for n, part in enumerate(parts):
                for q in range(per_part):
                    at = 2 * (part * per_part + q)
                    left = pl.multiple_of(codes_smem[r, at] * LANES, LANES)
                    right = pl.multiple_of(codes_smem[r, at + 1] * LANES, LANES)
                    to = n * width + q * LANES
                    spread_ref[pl.ds(first, blocksize), to : to + LANES] = jnp.where(
                        low_half,
                        tiles_ref[r, :, pl.ds(left, LANES)],
                        tiles_ref[r, :, pl.ds(right, LANES)],
                    )
            return carry

        lax.fori_loop(0, per_chunk, place, 0)
    step = 256
    for n, out in enumerate(outs):
        for t in range(width // step):
            at = n * width + t * step
            out[:, t * step : (t + 1) * step] = jnp.dot(
                margin_ref[...], spread_ref[:, at : at + step], preferred_element_type=jnp.float32
            )


def first_kernel(
    total_blocks,
    base_ref,
    labels_hbm,
    cols_hbm,
    scores_hbm,
    weights_hbm,
    down_ref,
    margin_ref,
    codes_ref,
    labels_ref,
    cols_ref,
    scores_ref,
    tiles_ref,
    spread_ref,
    codes_smem,
    small_sems,
    sems,
):
    cols_copy = pltpu.make_async_copy(cols_hbm, cols_ref, small_sems.at[0])
    labels_copy = pltpu.make_async_copy(labels_hbm, labels_ref, small_sems.at[1])
    scores_copy = pltpu.make_async_copy(scores_hbm, scores_ref, small_sems.at[2])
    cols_copy.start()
    labels_copy.start()
    scores_copy.start()
    copies = start_weights(weights_hbm, tiles_ref, sems)
    block_rows, blocksize, packed = weights_hbm.shape
    classes, samples, width = scores_ref.shape
    cols_copy.wait()
    codes_ref[...] = make_codes(
        cols_ref[...], base_ref[0], total_blocks, packed // LANES
    )
    codes_copy = pltpu.make_async_copy(codes_ref, codes_smem, small_sems.at[3])
    codes_copy.start()
    labels_copy.wait()
    row = lax.broadcasted_iota(jnp.int32, (samples, width), 0)
    labels = jnp.zeros((samples, width), jnp.int32)
    for s in range(samples):
        labels = jnp.where(row == s, labels_ref[s], labels)
    scores_copy.wait()
    scores = [scores_ref[c].astype(jnp.float32) for c in range(classes)]
    top = scores[0]
    for c in range(1, classes):
        top = jnp.where(labels == c, scores[c], top)
    for j in range(classes - 1):
        rest = jnp.where(labels > j, scores[j], scores[j + 1])
        margin_ref[pl.ds(j * samples, samples), :] = (top - rest).astype(jnp.bfloat16)
    codes_copy.wait()
    place_and_multiply(tiles_ref, spread_ref, codes_smem, margin_ref, copies, (0,), (down_ref,))


def first(total_blocks, base, labels, cols, scores, weights):
    classes, samples, width = scores.shape
    rows = (classes - 1) * samples
    block_rows, blocksize, packed = weights.shape
    hbm = pl.BlockSpec(memory_space=pltpu.HBM)
    vmem = pl.BlockSpec(memory_space=pltpu.VMEM)
    return pl.pallas_call(
        functools.partial(first_kernel, total_blocks),
        out_shape=(
            jax.ShapeDtypeStruct((rows, width), jnp.float32),
            jax.ShapeDtypeStruct((rows, width), jnp.bfloat16),
            jax.ShapeDtypeStruct((block_rows, LANES), jnp.int32),
        ),
        in_specs=[pl.BlockSpec(memory_space=pltpu.SMEM), hbm, hbm, hbm, hbm],
        out_specs=(vmem, vmem, vmem),
        scratch_shapes=[
            pltpu.SMEM((samples,), jnp.int32),
            pltpu.VMEM(cols.shape, jnp.int32),
            pltpu.VMEM(scores.shape, jnp.bfloat16),
            pltpu.VMEM((block_rows, blocksize, 2 * packed + LANES), jnp.bfloat16),
            pltpu.VMEM((block_rows * blocksize, width), jnp.bfloat16),
            pltpu.SMEM((block_rows, LANES), jnp.int32),
            pltpu.SemaphoreType.DMA((4,)),
            pltpu.SemaphoreType.DMA((CHUNKS,)),
        ],
        compiler_params=pltpu.CompilerParams(vmem_limit_bytes=61 << 20),
        cost_estimate=pl.CostEstimate(
            flops=2 * rows * width * width, bytes_accessed=6 << 20, transcendentals=0
        ),
        name="first",
    )(base, labels, cols, scores, weights)


def second_kernel(
    codes_hbm, bias_ref, margin_ref, weights_hbm, up_ref, centre_ref, bias_acc_ref, tiles_ref, spread_ref, codes_smem, small_sems, sems
):
    codes_copy = pltpu.make_async_copy(codes_hbm, codes_smem, small_sems.at[0])
    codes_copy.start()
    copies = start_weights(weights_hbm, tiles_ref, sems)
    width = margin_ref.shape[1]
    terms = margin_ref[...].astype(jnp.float32) * bias_ref[...]
    acc = terms[:, :LANES]
    for t in range(1, width // LANES):
        acc = acc + terms[:, t * LANES : (t + 1) * LANES]
    bias_acc_ref[...] = acc
    codes_copy.wait()
    place_and_multiply(tiles_ref, spread_ref, codes_smem, margin_ref, copies, (2, 1), (up_ref, centre_ref))


def second(codes, bias, margin, weights):
    rows, width = margin.shape
    block_rows, blocksize, packed = weights.shape
    hbm = pl.BlockSpec(memory_space=pltpu.HBM)
    vmem = pl.BlockSpec(memory_space=pltpu.VMEM)
    part = jax.ShapeDtypeStruct((rows, width), jnp.float32)
    return pl.pallas_call(
        second_kernel,
        out_shape=(part, part, jax.ShapeDtypeStruct((rows, LANES), jnp.float32)),
        in_specs=[vmem, vmem, vmem, hbm],
        out_specs=(vmem, vmem, vmem),
        scratch_shapes=[
            pltpu.VMEM((block_rows, blocksize, 2 * packed + LANES), jnp.bfloat16),
            pltpu.VMEM((block_rows * blocksize, 2 * width), jnp.bfloat16),
            pltpu.SMEM((block_rows, LANES), jnp.int32),
            pltpu.SemaphoreType.DMA((1,)),
            pltpu.SemaphoreType.DMA((CHUNKS,)),
        ],
        compiler_params=pltpu.CompilerParams(vmem_limit_bytes=30 << 20),
        cost_estimate=pl.CostEstimate(
            flops=4 * rows * width * width, bytes_accessed=6 << 20, transcendentals=0
        ),
        name="second",
    )(codes, bias, margin, weights)


def relax_kernel(
    flags_ref,
    mid_ref,
    rad_ref,
    slope_ref,
    bias_acc_ref,
    centre_ref,
    higher_ref,
    lower_ref,
    coef_ref,
    offs_ref,
    acc_ref,
):
    specs, samples, width = coef_ref.shape
    blocksize = width // flags_ref.shape[0]
    lower = mid_ref[...] - rad_ref[...]
    upper = mid_ref[...] + rad_ref[...]
    up_slope = (jnp.maximum(upper, 0.0) - jnp.maximum(lower, 0.0)) / (upper - lower)
    up_shift = jnp.maximum(lower, 0.0) - up_slope * lower
    block = lax.broadcasted_iota(jnp.int32, (1, width), 1) // blocksize
    flags = jnp.zeros((1, width), jnp.int32)
    for b in range(flags_ref.shape[0]):
        flags = jnp.where(block == b, flags_ref[b], flags)
    low_slope = jnp.where(flags == 1, slope_ref[...], up_slope)
    for j in range(specs):
        at = slice(j * samples, (j + 1) * samples)
        propagated = centre_ref[at] + higher_ref[at] + lower_ref[at]
        negative = jnp.minimum(propagated, 0.0)
        coef_ref[j] = (low_slope * jnp.maximum(propagated, 0.0) + up_slope * negative).astype(jnp.bfloat16)
        terms = negative * up_shift
        acc = bias_acc_ref[at]
        for t in range(width // LANES):
            acc = acc + terms[:, t * LANES : (t + 1) * LANES]
        acc_ref[at] = acc
    sums = lax.dot_general(
        jnp.ones((8, LANES), jnp.float32),
        acc_ref[...],
        (((1,), (1,)), ((), ())),
        precision=lax.Precision.HIGHEST,
        preferred_element_type=jnp.float32,
    )
    for d in range(offs_ref.shape[0]):
        offs_ref[d] = sums[:1]


def relax(flags, mid, rad, slope, bias_acc, centre, higher, lower, samples, devices):
    rows, width = centre.shape
    specs = rows // samples
    smem = pl.BlockSpec(memory_space=pltpu.SMEM)
    vmem = pl.BlockSpec(memory_space=pltpu.VMEM)
    return pl.pallas_call(
        relax_kernel,
        out_shape=(
            jax.ShapeDtypeStruct((specs, samples, width), jnp.bfloat16),
            jax.ShapeDtypeStruct((devices, 1, rows), jnp.float32),
        ),
        in_specs=[smem] + [vmem] * 7,
        out_specs=(vmem, vmem),
        scratch_shapes=[pltpu.VMEM((rows, LANES), jnp.float32)],
        compiler_params=pltpu.CompilerParams(vmem_limit_bytes=16 << 20),
        cost_estimate=pl.CostEstimate(
            flops=10 * rows * width, bytes_accessed=4 << 20, transcendentals=0
        ),
        name="relax",
    )(flags, mid, rad, slope, bias_acc, centre, higher, lower)


def total_kernel(parts_ref, out_ref):
    specs, samples = out_ref.shape
    sums = parts_ref[0]
    for d in range(1, parts_ref.shape[0]):
        sums = sums + parts_ref[d]
    for j in range(specs):
        out_ref[j : j + 1, :] = sums[:, j * samples : (j + 1) * samples]


def local(
    class_scores,
    true_class,
    weight_blocks,
    col_blocks,
    layer_bias,
    bound_mid,
    bound_rad,
    lower_slope,
    unstable_blocks,
):
    samples, classes, width = class_scores.shape
    specs = classes - 1
    per_dev = col_blocks.shape[0]
    devices = lax.axis_size("neuron")
    base = ((lax.axis_index("neuron") - 1) * per_dev).astype(jnp.int32).reshape(1)
    down, margin, codes = first(
        devices * per_dev,
        base, true_class, col_blocks, jnp.transpose(class_scores, (1, 0, 2)), weight_blocks
    )
    higher = shift_by(down, "neuron", -1)
    layer_bias, margin = lax.optimization_barrier((layer_bias, margin))
    bias = layer_bias.astype(jnp.float32).reshape(1, width)
    up, centre, bias_acc = second(codes, bias, margin, weight_blocks)
    lower = shift_by(up, "neuron", 1)
    coef, offs = relax(
        unstable_blocks,
        bound_mid.reshape(1, width),
        bound_rad.reshape(1, width),
        lower_slope.reshape(1, width),
        bias_acc,
        centre,
        higher,
        lower,
        samples,
        devices,
    )
    gathered = lax.all_to_all(offs, "neuron", 0, 0)
    offsets = pl.pallas_call(
        total_kernel,
        out_shape=jax.ShapeDtypeStruct((specs, samples), jnp.float32),
        name="total",
    )(gathered)
    return jnp.transpose(coef, (1, 0, 2)), offsets.T


def solution(mesh):
    placed = (
        P("spec", None, "neuron"),
        P("spec"),
        P("neuron", None, None),
        P("neuron", None),
        P("neuron"),
        P("neuron"),
        P("neuron"),
        P("neuron"),
        P("neuron"),
    )
    return jax.shard_map(
        local,
        mesh=mesh,
        in_specs=placed,
        out_specs=(P("spec", None, "neuron"), P("spec", None)),
        check_vma=False,
    )
```

time: 93.6 us -> 88.2 us (0.942)
  waiting for transfers between devices: 36.7 us -> 29.8 us
  local copies, waits for them, and re-layouts: 7.74 us -> 3.91 us
  blocking collectives: 18.3 us -> 20.9 us
  Pallas kernels: 12.6 us -> 15.1 us
    ppermute x2, waiting for transfers between devices: 36.7 us -> 29.8 us  [shift_by(): lax.ppermute(value, axis, [(i, (i + by) % length) for i in range(length)])]
    unnamed x16, local copies, waits for them, and re-layouts: 7.06 us -> 3.91 us
    all_to_all x1, blocking collectives: 18.3 us -> 20.9 us  [local(): gathered = lax.all_to_all(offs, 'neuron', 0, 0)]
    pallas_call x2 -> x3, Pallas kernels: 11.1 us -> 13.7 us  [the longest x1 6.59 us: first(): pl.pallas_call(functools.partial(first_kernel, total_blocks), out_shape=(...]
  transfers between devices with their start and end apart: 2 -> 2, of which waited for: 2 -> 2; matrix products, arithmetic and copies ran while one was open for 0% -> 0% of each run, Pallas kernels for 0% -> 6%
where the time goes in v2:
time: 88.2 us; the launch traced here: 87.8 us
  waiting for transfers between devices  29.8 us (34%)
  blocking collectives  20.9 us (24%)
  starting transfers between devices  17.3 us (20%)
  Pallas kernels  15.1 us (17%)
  local copies, waits for them, and re-layouts  3.91 us (4%)
    ppermute x2, waiting for transfers between devices, shift_by(): lax.ppermute(value, axis, [(i, (i + by) % length) for i in range(length)])  29.8 us
    all_to_all x1, blocking collectives, local(): gathered = lax.all_to_all(offs, 'neuron', 0, 0)  20.9 us
    ppermute x2, starting transfers between devices, shift_by(): lax.ppermute(value, axis, [(i, (i + by) % length) for i in range(length)])  17.3 us
    pallas_call x1, Pallas kernels, first(): pl.pallas_call(functools.partial(first_kernel, total_blocks), out_shape=(...  6.59 us
    pallas_call x1, Pallas kernels, second(): pl.pallas_call(second_kernel, out_shape=(part, part, jax.ShapeDtypeStruct...  5.22 us
    unnamed x16, local copies, waits for them, and re-layouts  3.91 us
    pallas_call x1, Pallas kernels, relax(): pl.pallas_call(relax_kernel, out_shape=(jax.ShapeDtypeStruct((specs, samp...  1.85 us
  transfers between devices with their start and end apart: 2, of which 2 were waited for; matrix products, arithmetic and copies ran while one was open for 0% of the time, Pallas kernels for 6%

profile of v2, /device:TPU:24, one launch (start us, length us, event | category | flops | bytes accessed | tf_op | source)
XLA Modules:
  0.0 87.8 jit_solution(2581430158269274033)
XLA Ops:
  0.6 0.0 copy-start.7
  0.6 0.0 copy-start.3
  0.7 0.0 copy-start.4
  0.7 0.0 copy-start.5
  0.7 0.0 copy-start.6
  0.7 6.6 %first.1 = (f32[216,1024]{1,0:T(8,128)}, bf16[216,1024]{1,0:T(8,128)(2,1)}, s32[16,128]{1,0:T(8,128)}) custom-call(s32[1]{0:T(128)} %bitcast.3.base_ref, s32[24]{0:T(128)} %labels_hbm.1, s32[16,32]{1,0:T(8,128)} %cols_hbm.1, bf16[10,24,1024]{2,1,0:T(8,128)(2,1)} %bitcast.12, bf16[16,64,2048]{2,1,0:T(8,128)(2,1)} %weights_hbm.3), custom_call_target="tpu_custom_call" | custom-call | flops 452984832 | bytes 6291456 | tf_op jit(solution)/shard_map/first/pallas_call | solution.py:148
  7.3 15.4 %collective-permute-start = (f32[216,1024]{1,0:T(8,128)}, f32[216,1024]{1,0:T(8,128)S(1)}, u32[]{:S(2)}, u32[]{:S(2)}) collective-permute-start(f32[216,1024]{1,0:T(8,128)} %get-tuple-element.18), channel_id=1, source_target_pairs={{0,31},{1,0},{2,1},{3,2},{4,3},{5,4},{6,5},{7,6},{8,7},{9,8},{10,9... | collective-permute-start | bytes 2654216 | tf_op jit(solution)/shard_map/ppermute | solution.py:16
  22.7 0.0 copy-done.7
  22.7 0.0 copy-start
  22.7 2.2 %copy-done = bf16[16,64,2048]{2,1,0:T(8,128)(2,1)S(1)} copy-done((bf16[16,64,2048]{2,1,0:T(8,128)(2,1)S(1)}, bf16[16,64,2048]{2,1,0:T(8,128)(2,1)}, u32[]{:S(2)}) %copy-start) | copy-done | bytes 4194328
  24.9 0.0 copy-start.1
  24.9 1.0 %copy-done.1 = bf16[216,1024]{1,0:T(8,128)(2,1)S(1)} copy-done((bf16[216,1024]{1,0:T(8,128)(2,1)S(1)}, bf16[216,1024]{1,0:T(8,128)(2,1)}, u32[]{:S(2)}) %copy-start.1) | copy-done | bytes 442392
  25.9 0.0 copy-start.2
  25.9 0.7 copy-done.2
  26.6 5.2 %second.1 = (f32[216,1024]{1,0:T(8,128)S(1)}, f32[216,1024]{1,0:T(8,128)S(1)}, f32[216,128]{1,0:T(8,128)S(1)}) custom-call(s32[16,128]{1,0:T(8,128)S(1)} %copy-done.2, f32[1,1024]{1,0:T(1,128)S(1)} %bitcast.8, bf16[216,1024]{1,0:T(8,128)(2,1)S(1)} %copy-done.1, bf16[16,64,2048]{2,1,0:T(8,128)(2,1)S(1)} %copy-done), custom_call_target="tpu_custom_call" | custom-call | flops 905969664 | bytes 6291456 | tf_op jit(solution)/shard_map/second/pallas_call | solution.py:197
  31.8 1.9 %collective-permute-start.1 = (f32[216,1024]{1,0:T(8,128)S(1)}, f32[216,1024]{1,0:T(8,128)S(1)}, u32[]{:S(2)}, u32[]{:S(2)}) collective-permute-start(f32[216,1024]{1,0:T(8,128)S(1)} %get-tuple-element.19), channel_id=1, source_target_pairs={{0,1},{1,2},{2,3},{3,4},{4,5},{5,6},{6,7},{7,8},{8,9},{9,10},{10,1... | collective-permute-start | bytes 2654216 | tf_op jit(solution)/shard_map/ppermute | solution.py:16
  33.7 9.3 %collective-permute-done.higher_ref = f32[216,1024]{1,0:T(8,128)S(1)} collective-permute-done((f32[216,1024]{1,0:T(8,128)}, f32[216,1024]{1,0:T(8,128)S(1)}, u32[]{:S(2)}, u32[]{:S(2)}) %collective-permute-start) | collective-permute-done | bytes 884768 | tf_op jit(solution)/shard_map/ppermute | solution.py:16
  43.1 20.4 %collective-permute-done.1.lower_ref = f32[216,1024]{1,0:T(8,128)S(1)} collective-permute-done((f32[216,1024]{1,0:T(8,128)S(1)}, f32[216,1024]{1,0:T(8,128)S(1)}, u32[]{:S(2)}, u32[]{:S(2)}) %collective-permute-start.1) | collective-permute-done | bytes 884768 | tf_op jit(solution)/shard_map/ppermute | solution.py:16
  63.5 0.0 copy-done.3
  63.5 0.0 copy-done.4
  63.5 0.0 copy-done.5
  63.5 0.0 copy-done.6
  63.5 1.8 %relax.1 = (bf16[9,24,1024]{2,1,0:T(8,128)(2,1)}, f32[32,1,216]{2,1,0:T(1,128)S(1)}) custom-call(s32[16]{0:T(128)S(1)} %copy-done.6, f32[1,1024]{1,0:T(1,128)S(1)} %bitcast.9, f32[1,1024]{1,0:T(1,128)S(1)} %bitcast.10, f32[1,1024]{1,0:T(1,128)S(1)} %bitcast.11, f32[216,128]{1,0:T(8,128)S(1)} %get-tuple-element.16.bias_acc_ref, ...), custom_call_target="tpu_custom_call" | custom-call | flops 2211840 | bytes 4194304 | tf_op jit(solution)/shard_map/relax/pallas_call | solution.py:267
  65.4 20.9 %all_to_all.5.parts_ref = f32[32,1,216]{2,1,0:T(1,128)} all-to-all(f32[32,1,216]{2,1,0:T(1,128)S(1)} %get-tuple-element.21), channel_id=1, replica_groups=mesh['spec'=16,'neuron'=32] {'neuron'}, dimensions={0} | all-to-all | bytes 55296 | tf_op jit(solution)/shard_map/all_to_all | solution.py:330
  86.3 1.5 %total.1 = f32[9,24]{1,0:T(8,128)} custom-call(f32[32,1,216]{2,1,0:T(1,128)} %all_to_all.5.parts_ref), custom_call_target="tpu_custom_call" | custom-call | tf_op jit(solution)/shard_map/total/pallas_call | solution.py:331
  (1 shorter events, 0.0 us)
Async XLA Ops:
  0.6 22.0 %copy-start.7 = (bf16[1024]{0:T(1024)(128)(2,1)S(1)}, bf16[1024]{0:T(1024)(128)(2,1)}, u32[]{:S(2)}) copy-start(bf16[1024]{0:T(1024)(128)(2,1)} %param.13) | copy-start | bytes 6148
  0.6 62.9 %copy-start.3 = (f32[1024]{0:T(1024)S(1)}, f32[1024]{0:T(1024)}, u32[]{:S(2)}) copy-start(f32[1024]{0:T(1024)} %param.14) | copy-start | bytes 12292
  0.7 62.9 %copy-start.4 = (f32[1024]{0:T(1024)S(1)}, f32[1024]{0:T(1024)}, u32[]{:S(2)}) copy-start(f32[1024]{0:T(1024)} %param.15) | copy-start | bytes 12292
  0.7 62.9 %copy-start.5 = (f32[1024]{0:T(1024)S(1)}, f32[1024]{0:T(1024)}, u32[]{:S(2)}) copy-start(f32[1024]{0:T(1024)} %param.16) | copy-start | bytes 12292
  0.7 62.9 %copy-start.6 = (s32[16]{0:T(128)S(1)}, s32[16]{0:T(128)}, u32[]{:S(2)}) copy-start(s32[16]{0:T(128)} %flags_ref.1) | copy-start | bytes 196
  7.3 35.8 %collective-permute-start = (f32[216,1024]{1,0:T(8,128)}, f32[216,1024]{1,0:T(8,128)S(1)}, u32[]{:S(2)}, u32[]{:S(2)}) collective-permute-start(f32[216,1024]{1,0:T(8,128)} %get-tuple-element.18), channel_id=1, source_target_pairs={{0,31},{1,0},{2,1},{3,2},{4,3},{5,4},{6,5},{7,6},{8,7},{9,8},{10,9... | collective-permute-start | bytes 2654216 | tf_op jit(solution)/shard_map/ppermute | solution.py:16
  22.7 2.2 %copy-start = (bf16[16,64,2048]{2,1,0:T(8,128)(2,1)S(1)}, bf16[16,64,2048]{2,1,0:T(8,128)(2,1)}, u32[]{:S(2)}) copy-start(bf16[16,64,2048]{2,1,0:T(8,128)(2,1)} %weights_hbm.3) | copy-start | bytes 12582916
  24.9 1.0 %copy-start.1 = (bf16[216,1024]{1,0:T(8,128)(2,1)S(1)}, bf16[216,1024]{1,0:T(8,128)(2,1)}, u32[]{:S(2)}) copy-start(bf16[216,1024]{1,0:T(8,128)(2,1)} %get-tuple-element.15.margin_ref) | copy-start | bytes 1327108
  25.9 0.7 copy-start.2
  31.8 31.7 %collective-permute-start.1 = (f32[216,1024]{1,0:T(8,128)S(1)}, f32[216,1024]{1,0:T(8,128)S(1)}, u32[]{:S(2)}, u32[]{:S(2)}) collective-permute-start(f32[216,1024]{1,0:T(8,128)S(1)} %get-tuple-element.19), channel_id=1, source_target_pairs={{0,1},{1,2},{2,3},{3,4},{4,5},{5,6},{6,7},{7,8},{8,9},{9,10},{10,1... | collective-permute-start | bytes 2654216 | tf_op jit(solution)/shard_map/ppermute | solution.py:16

commit v3 on v2

--- a/solution.py
+++ b/solution.py
@@ -7,13 +7,16 @@
 from jax.experimental.pallas import tpu as pltpu
 from jax.sharding import PartitionSpec as P
 
+
 LANES = 128
-CHUNKS = 4
-
-
-def shift_by(value, axis, by):
-    length = lax.axis_size(axis)
-    return lax.ppermute(value, axis, [(i, (i + by) % length) for i in range(length)])
+CHUNKS = 2
+
+
+RUN = 8
+
+
+def send(value, pairs):
+    return lax.ppermute(value, "neuron", pairs)
 
 
 def start_weights(weights_hbm, tiles_ref, sems):
@@ -95,17 +98,22 @@
     cols_hbm,
     scores_hbm,
     weights_hbm,
-    down_ref,
-    margin_ref,
-    codes_ref,
+    down_hbm,
+    up_hbm,
+    margin_hbm,
+    codes_hbm,
     labels_ref,
     cols_ref,
     scores_ref,
     tiles_ref,
     spread_ref,
+    codes_ref,
     codes_smem,
+    margin_ref,
+    parts_ref,
     small_sems,
     sems,
+    part_sems,
 ):
     cols_copy = pltpu.make_async_copy(cols_hbm, cols_ref, small_sems.at[0])
     labels_copy = pltpu.make_async_copy(labels_hbm, labels_ref, small_sems.at[1])
@@ -116,12 +124,17 @@
     copies = start_weights(weights_hbm, tiles_ref, sems)
     block_rows, blocksize, packed = weights_hbm.shape
     classes, samples, width = scores_ref.shape
+    source_tiles = packed // LANES
+    turned_at = source_tiles + 1
+    per_chunk = block_rows // CHUNKS
+    depth = per_chunk * blocksize
+    tiles_ref[:, :, packed : packed + LANES] = jnp.zeros((block_rows, blocksize, LANES), jnp.bfloat16)
     cols_copy.wait()
-    codes_ref[...] = make_codes(
-        cols_ref[...], base_ref[0], total_blocks, packed // LANES
-    )
+    codes_ref[...] = make_codes(cols_ref[...], base_ref[0], total_blocks, source_tiles)
     codes_copy = pltpu.make_async_copy(codes_ref, codes_smem, small_sems.at[3])
     codes_copy.start()
+    codes_out = pltpu.make_async_copy(codes_ref, codes_hbm, small_sems.at[4])
+    codes_out.start()
     labels_copy.wait()
     row = lax.broadcasted_iota(jnp.int32, (samples, width), 0)
     labels = jnp.zeros((samples, width), jnp.int32)
@@ -135,8 +148,69 @@
     for j in range(classes - 1):
         rest = jnp.where(labels > j, scores[j], scores[j + 1])
         margin_ref[pl.ds(j * samples, samples), :] = (top - rest).astype(jnp.bfloat16)
-    codes_copy.wait()
-    place_and_multiply(tiles_ref, spread_ref, codes_smem, margin_ref, copies, (0,), (down_ref,))
+    margin_out = pltpu.make_async_copy(margin_ref, margin_hbm, small_sems.at[5])
+    margin_out.start()
+    low_half = lax.broadcasted_iota(jnp.int32, (blocksize, LANES), 1) < blocksize
+    per_part = width // LANES
+
+    def turn(r):
+        for t in range(source_tiles):
+            at = (turned_at + t) * LANES
+            tiles_ref[r, :, at : at + LANES] = pltpu.roll(
+                tiles_ref[r, :, t * LANES : (t + 1) * LANES], blocksize, 1
+            )
+
+    def place(c, i):
+        r = c * per_chunk + i
+        for n, part in enumerate((0, 2)):
+            for q in range(per_part):
+                at = 2 * (part * per_part + q)
+                left = pl.multiple_of(codes_smem[r, at] * LANES, LANES)
+                right = pl.multiple_of(codes_smem[r, at + 1] * LANES, LANES)
+                to = n * width + q * LANES
+                spread_ref[c, i * blocksize : (i + 1) * blocksize, to : to + LANES] = jnp.where(
+                    low_half,
+                    tiles_ref[r, :, pl.ds(left, LANES)],
+                    tiles_ref[r, :, pl.ds(right, LANES)],
+                )
+
+    outs = []
+
+    def multiply(c):
+        step = 256
+        for t in range(2 * width // step):
+            product = jnp.dot(
+                margin_ref[:, c * depth : (c + 1) * depth],
+                spread_ref[c, :, t * step : (t + 1) * step],
+                preferred_element_type=jnp.float32,
+            )
+            at = slice(t * step, (t + 1) * step)
+            parts_ref[:, at] = product if c == 0 else parts_ref[:, at] + product
+            if c == CHUNKS - 1:
+                to = down_hbm if t * step < width else up_hbm
+                out = pltpu.make_async_copy(
+                    parts_ref.at[:, pl.ds(t * step, step)],
+                    to.at[:, pl.ds(t * step % width, step)],
+                    part_sems.at[t],
+                )
+                out.start()
+                outs.append(out)
+
+    for c in range(CHUNKS):
+        copies[c].wait()
+        if c == 0:
+            for i in range(per_chunk):
+                turn(i)
+            codes_copy.wait()
+        else:
+            multiply(c - 1)
+            for i in range(per_chunk):
+                turn(c * per_chunk + i)
+        for i in range(per_chunk):
+            place(c, i)
+    multiply(CHUNKS - 1)
+    for copy in outs + [codes_out, margin_out]:
+        copy.wait()
 
 
 def first(total_blocks, base, labels, cols, scores, weights):
@@ -144,36 +218,40 @@
     rows = (classes - 1) * samples
     block_rows, blocksize, packed = weights.shape
     hbm = pl.BlockSpec(memory_space=pltpu.HBM)
-    vmem = pl.BlockSpec(memory_space=pltpu.VMEM)
     return pl.pallas_call(
         functools.partial(first_kernel, total_blocks),
         out_shape=(
+            jax.ShapeDtypeStruct((rows, width), jnp.float32),
             jax.ShapeDtypeStruct((rows, width), jnp.float32),
             jax.ShapeDtypeStruct((rows, width), jnp.bfloat16),
             jax.ShapeDtypeStruct((block_rows, LANES), jnp.int32),
         ),
         in_specs=[pl.BlockSpec(memory_space=pltpu.SMEM), hbm, hbm, hbm, hbm],
-        out_specs=(vmem, vmem, vmem),
+        out_specs=(hbm, hbm, hbm, hbm),
         scratch_shapes=[
             pltpu.SMEM((samples,), jnp.int32),
             pltpu.VMEM(cols.shape, jnp.int32),
             pltpu.VMEM(scores.shape, jnp.bfloat16),
             pltpu.VMEM((block_rows, blocksize, 2 * packed + LANES), jnp.bfloat16),
-            pltpu.VMEM((block_rows * blocksize, width), jnp.bfloat16),
+            pltpu.VMEM((CHUNKS, block_rows * blocksize // CHUNKS, 2 * width), jnp.bfloat16),
+            pltpu.VMEM((block_rows, LANES), jnp.int32),
             pltpu.SMEM((block_rows, LANES), jnp.int32),
-            pltpu.SemaphoreType.DMA((4,)),
+            pltpu.VMEM((rows, width), jnp.bfloat16),
+            pltpu.VMEM((rows, 2 * width), jnp.float32),
+            pltpu.SemaphoreType.DMA((6,)),
             pltpu.SemaphoreType.DMA((CHUNKS,)),
+            pltpu.SemaphoreType.DMA((2 * width // 256,)),
         ],
         compiler_params=pltpu.CompilerParams(vmem_limit_bytes=61 << 20),
         cost_estimate=pl.CostEstimate(
-            flops=2 * rows * width * width, bytes_accessed=6 << 20, transcendentals=0
+            flops=4 * rows * width * width, bytes_accessed=6 << 20, transcendentals=0
         ),
         name="first",
     )(base, labels, cols, scores, weights)
 
 
 def second_kernel(
-    codes_hbm, bias_ref, margin_ref, weights_hbm, up_ref, centre_ref, bias_acc_ref, tiles_ref, spread_ref, codes_smem, small_sems, sems
+    codes_hbm, bias_ref, margin_ref, weights_hbm, centre_ref, bias_acc_ref, tiles_ref, spread_ref, codes_smem, small_sems, sems
 ):
     codes_copy = pltpu.make_async_copy(codes_hbm, codes_smem, small_sems.at[0])
     codes_copy.start()
@@ -185,7 +263,7 @@
         acc = acc + terms[:, t * LANES : (t + 1) * LANES]
     bias_acc_ref[...] = acc
     codes_copy.wait()
-    place_and_multiply(tiles_ref, spread_ref, codes_smem, margin_ref, copies, (2, 1), (up_ref, centre_ref))
+    place_and_multiply(tiles_ref, spread_ref, codes_smem, margin_ref, copies, (1,), (centre_ref,))
 
 
 def second(codes, bias, margin, weights):
@@ -196,19 +274,19 @@
     part = jax.ShapeDtypeStruct((rows, width), jnp.float32)
     return pl.pallas_call(
         second_kernel,
-        out_shape=(part, part, jax.ShapeDtypeStruct((rows, LANES), jnp.float32)),
+        out_shape=(part, jax.ShapeDtypeStruct((rows, LANES), jnp.float32)),
         in_specs=[vmem, vmem, vmem, hbm],
-        out_specs=(vmem, vmem, vmem),
+        out_specs=(vmem, vmem),
         scratch_shapes=[
             pltpu.VMEM((block_rows, blocksize, 2 * packed + LANES), jnp.bfloat16),
-            pltpu.VMEM((block_rows * blocksize, 2 * width), jnp.bfloat16),
+            pltpu.VMEM((block_rows * blocksize, width), jnp.bfloat16),
             pltpu.SMEM((block_rows, LANES), jnp.int32),
             pltpu.SemaphoreType.DMA((1,)),
             pltpu.SemaphoreType.DMA((CHUNKS,)),
         ],
         compiler_params=pltpu.CompilerParams(vmem_limit_bytes=30 << 20),
         cost_estimate=pl.CostEstimate(
-            flops=4 * rows * width * width, bytes_accessed=6 << 20, transcendentals=0
+            flops=2 * rows * width * width, bytes_accessed=6 << 20, transcendentals=0
         ),
         name="second",
     )(codes, bias, margin, weights)
@@ -223,6 +301,7 @@
     centre_ref,
     higher_ref,
     lower_ref,
+    closing_ref,
     coef_ref,
     offs_ref,
     acc_ref,
@@ -240,7 +319,7 @@
     low_slope = jnp.where(flags == 1, slope_ref[...], up_slope)
     for j in range(specs):
         at = slice(j * samples, (j + 1) * samples)
-        propagated = centre_ref[at] + higher_ref[at] + lower_ref[at]
+        propagated = centre_ref[at] + higher_ref[at] + lower_ref[at] + closing_ref[at]
         negative = jnp.minimum(propagated, 0.0)
         coef_ref[j] = (low_slope * jnp.maximum(propagated, 0.0) + up_slope * negative).astype(jnp.bfloat16)
         terms = negative * up_shift
@@ -259,7 +338,7 @@
         offs_ref[d] = sums[:1]
 
 
-def relax(flags, mid, rad, slope, bias_acc, centre, higher, lower, samples, devices):
+def relax(flags, mid, rad, slope, bias_acc, centre, higher, lower, closing, samples, devices):
     rows, width = centre.shape
     specs = rows // samples
     smem = pl.BlockSpec(memory_space=pltpu.SMEM)
@@ -270,7 +349,7 @@
             jax.ShapeDtypeStruct((specs, samples, width), jnp.bfloat16),
             jax.ShapeDtypeStruct((devices, 1, rows), jnp.float32),
         ),
-        in_specs=[smem] + [vmem] * 7,
+        in_specs=[smem] + [vmem] * 8,
         out_specs=(vmem, vmem),
         scratch_shapes=[pltpu.VMEM((rows, LANES), jnp.float32)],
         compiler_params=pltpu.CompilerParams(vmem_limit_bytes=16 << 20),
@@ -278,7 +357,7 @@
             flops=10 * rows * width, bytes_accessed=4 << 20, transcendentals=0
         ),
         name="relax",
-    )(flags, mid, rad, slope, bias_acc, centre, higher, lower)
+    )(flags, mid, rad, slope, bias_acc, centre, higher, lower, closing)
 
 
 def total_kernel(parts_ref, out_ref):
@@ -305,16 +384,28 @@
     specs = classes - 1
     per_dev = col_blocks.shape[0]
     devices = lax.axis_size("neuron")
-    base = ((lax.axis_index("neuron") - 1) * per_dev).astype(jnp.int32).reshape(1)
-    down, margin, codes = first(
+    position = lax.axis_index("neuron")
+    base = ((position - 1) * per_dev).astype(jnp.int32).reshape(1)
+    down, up, margin, codes = first(
         devices * per_dev,
-        base, true_class, col_blocks, jnp.transpose(class_scores, (1, 0, 2)), weight_blocks
-    )
-    higher = shift_by(down, "neuron", -1)
-    layer_bias, margin = lax.optimization_barrier((layer_bias, margin))
+        base,
+        true_class,
+        col_blocks,
+        jnp.transpose(class_scores, (1, 0, 2)),
+        weight_blocks,
+    )
+    starts = range(0, devices, RUN)
+    ends = range(RUN - 1, devices, RUN)
+    higher = send(down, [(i, i - 1) for i in range(devices) if i not in starts])
+    lower = send(up, [(i, i + 1) for i in range(devices) if i not in ends])
+    outer = jnp.where(position % RUN == 0, down, up)
+    closing = send(
+        outer,
+        [(i, (i - 1) % devices) for i in starts] + [(i, (i + 1) % devices) for i in ends],
+    )
+    layer_bias, margin, weight_blocks = lax.optimization_barrier((layer_bias, margin, weight_blocks))
     bias = layer_bias.astype(jnp.float32).reshape(1, width)
-    up, centre, bias_acc = second(codes, bias, margin, weight_blocks)
-    lower = shift_by(up, "neuron", 1)
+    centre, bias_acc = second(codes, bias, margin, weight_blocks)
     coef, offs = relax(
         unstable_blocks,
         bound_mid.reshape(1, width),
@@ -324,6 +415,7 @@
         centre,
         higher,
         lower,
+        closing,
         samples,
         devices,
     )

time: 88.2 us -> 86.1 us (0.976)
  waiting for transfers between devices: 29.8 us -> 24.1 us
  starting transfers between devices: 17.3 us -> 21.2 us
  other arithmetic: 0.01 us -> 1.29 us
  Pallas kernels: 15.1 us -> 14.2 us
    ppermute x2 -> x3, waiting for transfers between devices: 29.8 us -> 24.1 us  [send(): return lax.ppermute(value, 'neuron', pairs)]
    ppermute x2 -> x3, starting transfers between devices: 17.3 us -> 21.2 us  [send(): return lax.ppermute(value, 'neuron', pairs)]
    select_n x0 -> x1, other arithmetic: none -> 1.29 us  [local(): outer = jnp.where(position % RUN == 0, down, up)]
    pallas_call x1, Pallas kernels: 5.22 us -> 4.15 us  [second(): pl.pallas_call(second_kernel, out_shape=(part, jax.ShapeDtypeStruct((rows...]
  transfers between devices with their start and end apart: 2 -> 3, of which waited for: 2 -> 3; matrix products, arithmetic and copies ran while one was open for 0% -> 0% of each run, Pallas kernels for 6% -> 5%
where the time goes in v3:
time: 86.1 us; the launch traced here: 85.7 us
  waiting for transfers between devices  24.1 us (28%)
  starting transfers between devices  21.2 us (25%)
  blocking collectives  20.1 us (23%)
  Pallas kernels  14.2 us (16%)
  local copies, waits for them, and re-layouts  3.92 us (5%)
  other arithmetic  1.29 us (1%)
    ppermute x3, waiting for transfers between devices, send(): return lax.ppermute(value, 'neuron', pairs)  24.1 us
    ppermute x3, starting transfers between devices, send(): return lax.ppermute(value, 'neuron', pairs)  21.2 us
    all_to_all x1, blocking collectives, local(): gathered = lax.all_to_all(offs, 'neuron', 0, 0)  20.1 us
    pallas_call x1, Pallas kernels, first(): pl.pallas_call(functools.partial(first_kernel, total_blocks), out_shape=(...  6.77 us
    pallas_call x1, Pallas kernels, second(): pl.pallas_call(second_kernel, out_shape=(part, jax.ShapeDtypeStruct((rows...  4.15 us
    unnamed x16, local copies, waits for them, and re-layouts  3.92 us
    pallas_call x1, Pallas kernels, relax(): pl.pallas_call(relax_kernel, out_shape=(jax.ShapeDtypeStruct((specs, samp...  1.85 us
  transfers between devices with their start and end apart: 3, of which 3 were waited for; matrix products, arithmetic and copies ran while one was open for 0% of the time, Pallas kernels for 5%

profile of v3, /device:TPU:24, one launch (start us, length us, event | category | flops | bytes accessed | tf_op | source)
XLA Modules:
  0.0 85.7 jit_solution(5080518934927394561)
XLA Ops:
  0.6 0.0 copy-start.7
  0.7 6.8 %first.1 = (f32[216,1024]{1,0:T(8,128)}, f32[216,1024]{1,0:T(8,128)}, bf16[216,1024]{1,0:T(8,128)(2,1)}, s32[16,128]{1,0:T(8,128)}) custom-call(s32[1]{0:T(128)} %bitcast.3.base_ref, s32[24]{0:T(128)} %labels_hbm.1, s32[16,32]{1,0:T(8,128)} %cols_hbm.1, bf16[10,24,1024]{2,1,0:T(8,128)(2,1)} %bitcast.12, bf16[16,64,2048]{2,1,0:T(8,128)(2,1)} %weights_hbm.2), custom_call_target="tpu_custom_call" | custom-call | flops 905969664 | bytes 6291456 | tf_op jit(solution)/shard_map/first/pallas_call | solution.py:221
  7.4 0.0 copy-start.3
  7.4 0.0 copy-start.4
  7.5 0.0 copy-start.5
  7.5 0.0 copy-start.6
  7.5 1.3 %broadcast_select_fusion = f32[216,1024]{1,0:T(8,128)S(1)} fusion(f32[216,1024]{1,0:T(8,128)} %get-tuple-element.20, f32[216,1024]{1,0:T(8,128)} %get-tuple-element.21, pred[]{:T(512)S(6)} %eq.5), kind=kLoop, calls=%fused_computation | loop fusion | flops 221184 | bytes 2654209 | tf_op jit(solution)/shard_map/jit(_where)/select_n | solution.py:401
  8.8 15.3 %collective-permute-start.2 = (f32[216,1024]{1,0:T(8,128)S(1)}, f32[216,1024]{1,0:T(8,128)S(1)}, u32[]{:S(2)}, u32[]{:S(2)}) collective-permute-start(f32[216,1024]{1,0:T(8,128)S(1)} %broadcast_select_fusion), channel_id=1, source_target_pairs={{0,31},{8,7},{16,15},{24,23},{7,8},{15,16},{23,24},{31,0},{32,63},... | collective-permute-start | bytes 2654216 | tf_op jit(solution)/shard_map/ppermute | solution.py:19
  24.1 1.3 %collective-permute-start = (f32[216,1024]{1,0:T(8,128)}, f32[216,1024]{1,0:T(8,128)S(1)}, u32[]{:S(2)}, u32[]{:S(2)}) collective-permute-start(f32[216,1024]{1,0:T(8,128)} %get-tuple-element.20), channel_id=1, source_target_pairs={{1,0},{2,1},{3,2},{4,3},{5,4},{6,5},{7,6},{9,8},{10,9},{11,10},{12... | collective-permute-start | bytes 2654216 | tf_op jit(solution)/shard_map/ppermute | solution.py:19
  25.4 4.6 %collective-permute-start.1 = (f32[216,1024]{1,0:T(8,128)}, f32[216,1024]{1,0:T(8,128)S(1)}, u32[]{:S(2)}, u32[]{:S(2)}) collective-permute-start(f32[216,1024]{1,0:T(8,128)} %get-tuple-element.21), channel_id=1, source_target_pairs={{0,1},{1,2},{2,3},{3,4},{4,5},{5,6},{6,7},{8,9},{9,10},{10,11},{11... | collective-permute-start | bytes 2654216 | tf_op jit(solution)/shard_map/ppermute | solution.py:19
  30.0 0.0 copy-done.7
  30.1 0.0 copy-start
  30.1 2.2 %copy-done = bf16[16,64,2048]{2,1,0:T(8,128)(2,1)S(1)} copy-done((bf16[16,64,2048]{2,1,0:T(8,128)(2,1)S(1)}, bf16[16,64,2048]{2,1,0:T(8,128)(2,1)}, u32[]{:S(2)}) %copy-start) | copy-done | bytes 4194328
  32.3 0.0 copy-start.1
  32.3 1.0 %copy-done.1 = bf16[216,1024]{1,0:T(8,128)(2,1)S(1)} copy-done((bf16[216,1024]{1,0:T(8,128)(2,1)S(1)}, bf16[216,1024]{1,0:T(8,128)(2,1)}, u32[]{:S(2)}) %copy-start.1) | copy-done | bytes 442392
  33.3 0.0 copy-start.2
  33.3 0.7 copy-done.2
  34.0 4.1 %second.1 = (f32[216,1024]{1,0:T(8,128)S(1)}, f32[216,128]{1,0:T(8,128)S(1)}) custom-call(s32[16,128]{1,0:T(8,128)S(1)} %copy-done.2, f32[1,1024]{1,0:T(1,128)S(1)} %bitcast.8, bf16[216,1024]{1,0:T(8,128)(2,1)S(1)} %copy-done.1, bf16[16,64,2048]{2,1,0:T(8,128)(2,1)S(1)} %copy-done), custom_call_target="tpu_custom_call" | custom-call | flops 452984832 | bytes 6291456 | tf_op jit(solution)/shard_map/second/pallas_call | solution.py:275
  38.1 6.6 %collective-permute-done.2.closing_ref = f32[216,1024]{1,0:T(8,128)S(1)} collective-permute-done((f32[216,1024]{1,0:T(8,128)S(1)}, f32[216,1024]{1,0:T(8,128)S(1)}, u32[]{:S(2)}, u32[]{:S(2)}) %collective-permute-start.2) | collective-permute-done | bytes 884768 | tf_op jit(solution)/shard_map/ppermute | solution.py:19
  44.7 16.0 %collective-permute-done.higher_ref = f32[216,1024]{1,0:T(8,128)S(1)} collective-permute-done((f32[216,1024]{1,0:T(8,128)}, f32[216,1024]{1,0:T(8,128)S(1)}, u32[]{:S(2)}, u32[]{:S(2)}) %collective-permute-start) | collective-permute-done | bytes 884768 | tf_op jit(solution)/shard_map/ppermute | solution.py:19
  60.6 1.5 %collective-permute-done.1.lower_ref = f32[216,1024]{1,0:T(8,128)S(1)} collective-permute-done((f32[216,1024]{1,0:T(8,128)}, f32[216,1024]{1,0:T(8,128)S(1)}, u32[]{:S(2)}, u32[]{:S(2)}) %collective-permute-start.1) | collective-permute-done | bytes 884768 | tf_op jit(solution)/shard_map/ppermute | solution.py:19
  62.2 0.0 copy-done.3
  62.2 0.0 copy-done.4
  62.2 0.0 copy-done.5
  62.2 0.0 copy-done.6
  62.2 1.9 %relax.1 = (bf16[9,24,1024]{2,1,0:T(8,128)(2,1)}, f32[32,1,216]{2,1,0:T(1,128)S(1)}) custom-call(s32[16]{0:T(128)S(1)} %copy-done.6, f32[1,1024]{1,0:T(1,128)S(1)} %bitcast.9, f32[1,1024]{1,0:T(1,128)S(1)} %bitcast.10, f32[1,1024]{1,0:T(1,128)S(1)} %bitcast.11, f32[216,128]{1,0:T(8,128)S(1)} %get-tuple-element.18.bias_acc_ref, ...), custom_call_target="tpu_custom_call" | custom-call | flops 2211840 | bytes 4194304 | tf_op jit(solution)/shard_map/relax/pallas_call | solution.py:346
  64.0 20.1 %all_to_all.5.parts_ref = f32[32,1,216]{2,1,0:T(1,128)} all-to-all(f32[32,1,216]{2,1,0:T(1,128)S(1)} %get-tuple-element.23), channel_id=1, replica_groups=mesh['spec'=16,'neuron'=32] {'neuron'}, dimensions={0} | all-to-all | bytes 55296 | tf_op jit(solution)/shard_map/all_to_all | solution.py:422
  84.2 1.5 %total.1 = f32[9,24]{1,0:T(8,128)} custom-call(f32[32,1,216]{2,1,0:T(1,128)} %all_to_all.5.parts_ref), custom_call_target="tpu_custom_call" | custom-call | tf_op jit(solution)/shard_map/total/pallas_call | solution.py:423
  (1 shorter events, 0.0 us)
Async XLA Ops:
  0.6 29.4 %copy-start.7 = (bf16[1024]{0:T(1024)(128)(2,1)S(1)}, bf16[1024]{0:T(1024)(128)(2,1)}, u32[]{:S(2)}) copy-start(bf16[1024]{0:T(1024)(128)(2,1)} %param.13) | copy-start | bytes 6148
  7.4 54.7 %copy-start.3 = (f32[1024]{0:T(1024)S(1)}, f32[1024]{0:T(1024)}, u32[]{:S(2)}) copy-start(f32[1024]{0:T(1024)} %param.14) | copy-start | bytes 12292
  7.4 54.7 %copy-start.4 = (f32[1024]{0:T(1024)S(1)}, f32[1024]{0:T(1024)}, u32[]{:S(2)}) copy-start(f32[1024]{0:T(1024)} %param.15) | copy-start | bytes 12292
  7.5 54.7 %copy-start.5 = (f32[1024]{0:T(1024)S(1)}, f32[1024]{0:T(1024)}, u32[]{:S(2)}) copy-start(f32[1024]{0:T(1024)} %param.16) | copy-start | bytes 12292
  7.5 54.7 %copy-start.6 = (s32[16]{0:T(128)S(1)}, s32[16]{0:T(128)}, u32[]{:S(2)}) copy-start(s32[16]{0:T(128)} %flags_ref.1) | copy-start | bytes 196
  8.8 35.9 %collective-permute-start.2 = (f32[216,1024]{1,0:T(8,128)S(1)}, f32[216,1024]{1,0:T(8,128)S(1)}, u32[]{:S(2)}, u32[]{:S(2)}) collective-permute-start(f32[216,1024]{1,0:T(8,128)S(1)} %broadcast_select_fusion), channel_id=1, source_target_pairs={{0,31},{8,7},{16,15},{24,23},{7,8},{15,16},{23,24},{31,0},{32,63},... | collective-permute-start | bytes 2654216 | tf_op jit(solution)/shard_map/ppermute | solution.py:19
  24.1 36.5 %collective-permute-start = (f32[216,1024]{1,0:T(8,128)}, f32[216,1024]{1,0:T(8,128)S(1)}, u32[]{:S(2)}, u32[]{:S(2)}) collective-permute-start(f32[216,1024]{1,0:T(8,128)} %get-tuple-element.20), channel_id=1, source_target_pairs={{1,0},{2,1},{3,2},{4,3},{5,4},{6,5},{7,6},{9,8},{10,9},{11,10},{12... | collective-permute-start | bytes 2654216 | tf_op jit(solution)/shard_map/ppermute | solution.py:19
  25.4 36.7 %collective-permute-start.1 = (f32[216,1024]{1,0:T(8,128)}, f32[216,1024]{1,0:T(8,128)S(1)}, u32[]{:S(2)}, u32[]{:S(2)}) collective-permute-start(f32[216,1024]{1,0:T(8,128)} %get-tuple-element.21), channel_id=1, source_target_pairs={{0,1},{1,2},{2,3},{3,4},{4,5},{5,6},{6,7},{8,9},{9,10},{10,11},{11... | collective-permute-start | bytes 2654216 | tf_op jit(solution)/shard_map/ppermute | solution.py:19
  30.1 2.2 %copy-start = (bf16[16,64,2048]{2,1,0:T(8,128)(2,1)S(1)}, bf16[16,64,2048]{2,1,0:T(8,128)(2,1)}, u32[]{:S(2)}) copy-start(bf16[16,64,2048]{2,1,0:T(8,128)(2,1)} %weights_hbm.2) | copy-start | bytes 12582916
  32.3 1.0 %copy-start.1 = (bf16[216,1024]{1,0:T(8,128)(2,1)S(1)}, bf16[216,1024]{1,0:T(8,128)(2,1)}, u32[]{:S(2)}) copy-start(bf16[216,1024]{1,0:T(8,128)(2,1)} %get-tuple-element.16.margin_ref) | copy-start | bytes 1327108
  33.3 0.7 copy-start.2

commit v4 on v2

v4 whole, which is shorter than its diff:
```python
import functools

import jax
import jax.numpy as jnp
from jax import lax
from jax.experimental import pallas as pl
from jax.experimental.pallas import tpu as pltpu
from jax.sharding import PartitionSpec as P


LANES = 128
CHUNKS = 2


RUN = 8


def send(value, pairs):
    return lax.ppermute(value, "neuron", pairs)


def start_weights(weights_hbm, tiles_ref, sems):
    block_rows, _, packed = weights_hbm.shape
    copies = [
        pltpu.make_async_copy(
            weights_hbm.at[r], tiles_ref.at[:, pl.ds(2 * packed * r, packed)], sems.at[r]
        )
        for r in range(block_rows)
    ]
    for copy in copies:
        copy.start()
    return copies


def make_codes(cols, base, total_blocks, source_tiles):
    block_rows, kept = cols.shape
    positions = (cols - base) & (total_blocks - 1)
    slot = lax.broadcasted_iota(jnp.int32, (block_rows, LANES), 1)
    own = lax.broadcasted_iota(jnp.int32, (block_rows, LANES), 0) * (2 * source_tiles)
    found = jnp.full((block_rows, LANES), -1, jnp.int32)
    for k in range(kept):
        found = jnp.where(slot == positions[:, k : k + 1], k, found)
    same_half = (found & 1) == (slot & 1)
    tile = own + (found >> 1)
    held = jnp.where(same_half, tile, tile + source_tiles)
    return jnp.where(found < 0, 2 * source_tiles * block_rows, held)


def turn(tiles_ref, r, packed, blocksize):
    for t in range(packed // LANES):
        at = 2 * packed * r + t * LANES
        tiles_ref[:, at + packed : at + packed + LANES] = pltpu.roll(
            tiles_ref[:, at : at + LANES], blocksize, 1
        )


def place(tiles_ref, spread_ref, codes_smem, c, i, r, parts, width):
    blocksize = tiles_ref.shape[0]
    low_half = lax.broadcasted_iota(jnp.int32, (blocksize, LANES), 1) < blocksize
    per_part = width // LANES
    for n, part in enumerate(parts):
        for q in range(per_part):
            at = 2 * (part * per_part + q)
            left = pl.multiple_of(codes_smem[r, at] * LANES, LANES)
            right = pl.multiple_of(codes_smem[r, at + 1] * LANES, LANES)
            to = n * width + q * LANES
            spread_ref[c, i * blocksize : (i + 1) * blocksize, to : to + LANES] = jnp.where(
                low_half, tiles_ref[:, pl.ds(left, LANES)], tiles_ref[:, pl.ds(right, LANES)]
            )


def multiply(margin_ref, spread_ref, c, outs):
    depth, total = spread_ref.shape[1:]
    width = total // len(outs)
    step = 256
    for t in range(total // step):
        product = jnp.dot(
            margin_ref[:, c * depth : (c + 1) * depth],
            spread_ref[c, :, t * step : (t + 1) * step],
            preferred_element_type=jnp.float32,
        )
        out = outs[t * step // width]
        at = slice(t * step % width, t * step % width + step)
        out[:, at] = product if c == 0 else out[:, at] + product


def place_and_multiply(tiles_ref, spread_ref, codes_smem, codes_copy, margin_ref, copies, parts, outs):
    blocksize = tiles_ref.shape[0]
    block_rows = len(copies)
    packed = (tiles_ref.shape[1] - LANES) // (2 * block_rows)
    per_chunk = block_rows // CHUNKS
    width = margin_ref.shape[1]
    tiles_ref[:, tiles_ref.shape[1] - LANES :] = jnp.zeros((blocksize, LANES), jnp.bfloat16)
    for c in range(CHUNKS):
        rows = range(c * per_chunk, (c + 1) * per_chunk)
        for r in rows:
            copies[r].wait()
        if c > 0:
            multiply(margin_ref, spread_ref, c - 1, outs)
        for r in rows:
            turn(tiles_ref, r, packed, blocksize)
        if c == 0:
            codes_copy.wait()
        for i, r in enumerate(rows):
            place(tiles_ref, spread_ref, codes_smem, c, i, r, parts, width)
    multiply(margin_ref, spread_ref, CHUNKS - 1, outs)


def tile_scratch(weights, parts, width):
    block_rows, blocksize, packed = weights.shape
    return [
        pltpu.VMEM((blocksize, block_rows * 2 * packed + LANES), jnp.bfloat16),
        pltpu.VMEM((CHUNKS, block_rows * blocksize // CHUNKS, parts * width), jnp.bfloat16),
    ]


def first_kernel(
    total_blocks,
    base_ref,
    labels_hbm,
    cols_hbm,
    scores_hbm,
    weights_hbm,
    down_ref,
    up_ref,
    margin_hbm,
    codes_ref,
    labels_ref,
    cols_ref,
    scores_ref,
    margin_ref,
    tiles_ref,
    spread_ref,
    codes_smem,
    small_sems,
    sems,
):
    cols_copy = pltpu.make_async_copy(cols_hbm, cols_ref, small_sems.at[0])
    labels_copy = pltpu.make_async_copy(labels_hbm, labels_ref, small_sems.at[1])
    scores_copy = pltpu.make_async_copy(scores_hbm, scores_ref, small_sems.at[2])
    cols_copy.start()
    labels_copy.start()
    scores_copy.start()
    copies = start_weights(weights_hbm, tiles_ref, sems)
    classes, samples, width = scores_ref.shape
    cols_copy.wait()
    codes_ref[...] = make_codes(
        cols_ref[...], base_ref[0], total_blocks, weights_hbm.shape[2] // LANES
    )
    codes_copy = pltpu.make_async_copy(codes_ref, codes_smem, small_sems.at[3])
    codes_copy.start()
    labels_copy.wait()
    row = lax.broadcasted_iota(jnp.int32, (samples, width), 0)
    labels = jnp.zeros((samples, width), jnp.int32)
    for s in range(samples):
        labels = jnp.where(row == s, labels_ref[s], labels)
    scores_copy.wait()
    scores = [scores_ref[c].astype(jnp.float32) for c in range(classes)]
    top = scores[0]
    for c in range(1, classes):
        top = jnp.where(labels == c, scores[c], top)
    for j in range(classes - 1):
        rest = jnp.where(labels > j, scores[j], scores[j + 1])
        margin_ref[pl.ds(j * samples, samples), :] = (top - rest).astype(jnp.bfloat16)
    margin_copy = pltpu.make_async_copy(margin_ref, margin_hbm, small_sems.at[4])
    margin_copy.start()
    place_and_multiply(
        tiles_ref, spread_ref, codes_smem, codes_copy, margin_ref, copies, (0, 2), (down_ref, up_ref)
    )
    margin_copy.wait()


def first(total_blocks, base, labels, cols, scores, weights):
    classes, samples, width = scores.shape
    rows = (classes - 1) * samples
    block_rows = weights.shape[0]
    hbm = pl.BlockSpec(memory_space=pltpu.HBM)
    vmem = pl.BlockSpec(memory_space=pltpu.VMEM)
    return pl.pallas_call(
        functools.partial(first_kernel, total_blocks),
        out_shape=(
            pltpu.VMEM((rows, width), jnp.float32),
            pltpu.VMEM((rows, width), jnp.float32),
            jax.ShapeDtypeStruct((rows, width), jnp.bfloat16),
            pltpu.VMEM((block_rows, LANES), jnp.int32),
        ),
        in_specs=[pl.BlockSpec(memory_space=pltpu.SMEM), hbm, hbm, hbm, hbm],
        out_specs=(vmem, vmem, hbm, vmem),
        scratch_shapes=[
            pltpu.SMEM((samples,), jnp.int32),
            pltpu.VMEM(cols.shape, jnp.int32),
            pltpu.VMEM(scores.shape, jnp.bfloat16),
            pltpu.VMEM((rows, width), jnp.bfloat16),
            *tile_scratch(weights, 2, width),
            pltpu.SMEM((block_rows, LANES), jnp.int32),
            pltpu.SemaphoreType.DMA((5,)),
            pltpu.SemaphoreType.DMA((block_rows,)),
        ],
        compiler_params=pltpu.CompilerParams(vmem_limit_bytes=60 << 20),
        cost_estimate=pl.CostEstimate(
            flops=4 * rows * width * width, bytes_accessed=6 << 20, transcendentals=0
        ),
        name="first",
    )(base, labels, cols, scores, weights)


def second_kernel(
    flags_ref,
    codes_vmem,
    bias_ref,
    mid_ref,
    rad_ref,
    slope_ref,
    margin_hbm,
    weights_hbm,
    centre_ref,
    bias_acc_ref,
    slopes_ref,
    margin_ref,
    tiles_ref,
    spread_ref,
    codes_smem,
    small_sems,
    sems,
):
    codes_copy = pltpu.make_async_copy(codes_vmem, codes_smem, small_sems.at[0])
    codes_copy.start()
    margin_copy = pltpu.make_async_copy(margin_hbm, margin_ref, small_sems.at[1])
    margin_copy.start()
    copies = start_weights(weights_hbm, tiles_ref, sems)
    width = margin_ref.shape[1]
    margin_copy.wait()
    terms = margin_ref[...].astype(jnp.float32) * bias_ref[...]
    acc = terms[:, :LANES]
    for t in range(1, width // LANES):
        acc = acc + terms[:, t * LANES : (t + 1) * LANES]
    bias_acc_ref[...] = acc
    lower = mid_ref[...] - rad_ref[...]
    upper = mid_ref[...] + rad_ref[...]
    up_slope = (jnp.maximum(upper, 0.0) - jnp.maximum(lower, 0.0)) / (upper - lower)
    blocks = flags_ref.shape[0]
    block = lax.broadcasted_iota(jnp.int32, (1, width), 1) // (width // blocks)
    flags = jnp.zeros((1, width), jnp.int32)
    for b in range(blocks):
        flags = jnp.where(block == b, flags_ref[b], flags)
    slopes_ref[0:1] = jnp.where(flags == 1, slope_ref[...], up_slope)
    slopes_ref[1:2] = up_slope
    slopes_ref[2:3] = jnp.maximum(lower, 0.0) - up_slope * lower
    place_and_multiply(
        tiles_ref, spread_ref, codes_smem, codes_copy, margin_ref, copies, (1,), (centre_ref,)
    )


def second(flags, codes, bias, mid, rad, slope, margin, weights):
    rows, width = margin.shape
    block_rows = weights.shape[0]
    vmem = pl.BlockSpec(memory_space=pltpu.VMEM)
    return pl.pallas_call(
        second_kernel,
        out_shape=(
            pltpu.VMEM((rows, width), jnp.float32),
            pltpu.VMEM((rows, LANES), jnp.float32),
            pltpu.VMEM((3, width), jnp.float32),
        ),
        in_specs=[pl.BlockSpec(memory_space=pltpu.SMEM)]
        + [vmem] * 5
        + [pl.BlockSpec(memory_space=pltpu.HBM)] * 2,
        out_specs=(vmem, vmem, vmem),
        scratch_shapes=[
            pltpu.VMEM((rows, width), jnp.bfloat16),
            *tile_scratch(weights, 1, width),
            pltpu.SMEM((block_rows, LANES), jnp.int32),
            pltpu.SemaphoreType.DMA((2,)),
            pltpu.SemaphoreType.DMA((block_rows,)),
        ],
        compiler_params=pltpu.CompilerParams(vmem_limit_bytes=30 << 20),
        cost_estimate=pl.CostEstimate(
            flops=2 * rows * width * width, bytes_accessed=6 << 20, transcendentals=0
        ),
        name="second",
    )(flags, codes, bias, mid, rad, slope, margin, weights)


def sums_kernel(slopes_ref, bias_acc_ref, centre_ref, higher_ref, lower_ref, closing_ref, offs_ref, acc_ref):
    rows, width = centre_ref.shape
    up_shift = slopes_ref[2:3]
    part = 24
    for first_row in range(0, rows, part):
        at = slice(first_row, first_row + part)
        propagated = centre_ref[at] + higher_ref[at] + lower_ref[at] + closing_ref[at]
        terms = jnp.minimum(propagated, 0.0) * up_shift
        acc = bias_acc_ref[at]
        for t in range(width // LANES):
            acc = acc + terms[:, t * LANES : (t + 1) * LANES]
        acc_ref[at] = acc
    sums = lax.dot_general(
        jnp.ones((8, LANES), jnp.float32),
        acc_ref[...],
        (((1,), (1,)), ((), ())),
        precision=lax.Precision.HIGHEST,
        preferred_element_type=jnp.float32,
    )
    for d in range(offs_ref.shape[0]):
        offs_ref[d] = sums[:1]


def sums(devices, slopes, bias_acc, centre, higher, lower, closing):
    rows, _ = centre.shape
    vmem = pl.BlockSpec(memory_space=pltpu.VMEM)
    return pl.pallas_call(
        sums_kernel,
        out_shape=pltpu.VMEM((devices, 1, rows), jnp.float32),
        in_specs=[vmem] * 6,
        out_specs=vmem,
        scratch_shapes=[pltpu.VMEM((rows, LANES), jnp.float32)],
        compiler_params=pltpu.CompilerParams(vmem_limit_bytes=16 << 20),
        name="sums",
    )(slopes, bias_acc, centre, higher, lower, closing)


def last_kernel(
    slopes_ref,
    centre_ref,
    higher_ref,
    lower_ref,
    closing_ref,
    gathered_ref,
    coef_hbm,
    out_ref,
    coef_ref,
    coef_sems,
):
    specs, samples, _ = coef_ref.shape
    low_slope = slopes_ref[0:1]
    up_slope = slopes_ref[1:2]
    copies = []
    for j in range(specs):
        at = slice(j * samples, (j + 1) * samples)
        propagated = centre_ref[at] + higher_ref[at] + lower_ref[at] + closing_ref[at]
        positive = jnp.maximum(propagated, 0.0)
        negative = jnp.minimum(propagated, 0.0)
        coef_ref[j] = (low_slope * positive + up_slope * negative).astype(jnp.bfloat16)
        copies.append(pltpu.make_async_copy(coef_ref.at[j], coef_hbm.at[j], coef_sems.at[j]))
        copies[-1].start()
    total = gathered_ref[0]
    for d in range(1, gathered_ref.shape[0]):
        total = total + gathered_ref[d]
    for j in range(specs):
        out_ref[j : j + 1, :] = total[:, j * samples : (j + 1) * samples]
    for copy in copies:
        copy.wait()


def last(samples, slopes, centre, higher, lower, closing, gathered):
    rows, width = centre.shape
    specs = rows // samples
    vmem = pl.BlockSpec(memory_space=pltpu.VMEM)
    hbm = pl.BlockSpec(memory_space=pltpu.HBM)
    return pl.pallas_call(
        last_kernel,
        out_shape=(
            jax.ShapeDtypeStruct((specs, samples, width), jnp.bfloat16),
            jax.ShapeDtypeStruct((specs, samples), jnp.float32),
        ),
        in_specs=[vmem] * 6,
        out_specs=(hbm, vmem),
        scratch_shapes=[
            pltpu.VMEM((specs, samples, width), jnp.bfloat16),
            pltpu.SemaphoreType.DMA((specs,)),
        ],
        compiler_params=pltpu.CompilerParams(vmem_limit_bytes=16 << 20),
        name="last",
    )(slopes, centre, higher, lower, closing, gathered)


def local(
    class_scores,
    true_class,
    weight_blocks,
    col_blocks,
    layer_bias,
    bound_mid,
    bound_rad,
    lower_slope,
    unstable_blocks,
):
    samples, _, width = class_scores.shape
    per_dev = col_blocks.shape[0]
    devices = lax.axis_size("neuron")
    position = lax.axis_index("neuron")
    base = ((position - 1) * per_dev).astype(jnp.int32).reshape(1)
    down, up, margin, codes = first(
        devices * per_dev,
        base,
        true_class,
        col_blocks,
        jnp.transpose(class_scores, (1, 0, 2)),
        weight_blocks,
    )
    starts = range(0, devices, RUN)
    ends = range(RUN - 1, devices, RUN)
    higher = send(down, [(i, i - 1) for i in range(devices) if i not in starts])
    lower = send(up, [(i, i + 1) for i in range(devices) if i not in ends])
    outer = jnp.where(position % RUN == 0, down, up)
    closing = send(
        outer,
        [(i, (i - 1) % devices) for i in starts] + [(i, (i + 1) % devices) for i in ends],
    )
    bias = layer_bias.astype(jnp.float32).reshape(1, width)
    centre, bias_acc, slopes = second(
        unstable_blocks,
        codes,
        bias,
        bound_mid.reshape(1, width),
        bound_rad.reshape(1, width),
        lower_slope.reshape(1, width),
        margin,
        weight_blocks,
    )
    offs = sums(devices, slopes, bias_acc, centre, higher, lower, closing)
    gathered = lax.all_to_all(offs, "neuron", 0, 0)
    coef, offsets = last(samples, slopes, centre, higher, lower, closing, gathered)
    return jnp.transpose(coef, (1, 0, 2)), offsets.T


def solution(mesh):
    placed = (
        P("spec", None, "neuron"),
        P("spec"),
        P("neuron", None, None),
        P("neuron", None),
        P("neuron"),
        P("neuron"),
        P("neuron"),
        P("neuron"),
        P("neuron"),
    )
    return jax.shard_map(
        local,
        mesh=mesh,
        in_specs=placed,
        out_specs=(P("spec", None, "neuron"), P("spec", None)),
        check_vma=False,
    )
```

time: 88.2 us -> 82.4 us (0.934)
  waiting for transfers between devices: 29.8 us -> 25 us
  starting transfers between devices: 17.3 us -> 21.2 us
  Pallas kernels: 15.1 us -> 11.7 us
  blocking collectives: 20.9 us -> 20 us
    ppermute x2 -> x3, waiting for transfers between devices: 29.8 us -> 25 us  [send(): return lax.ppermute(value, 'neuron', pairs)]
    ppermute x2 -> x3, starting transfers between devices: 17.3 us -> 21.2 us  [send(): return lax.ppermute(value, 'neuron', pairs)]
    pallas_call x3, Pallas kernels: 8.54 us -> 5.78 us  [the longest x1 3.71 us: second(): pl.pallas_call(second_kernel, out_shape=(pltpu.VMEM((rows, width), jnp.fl...]
    all_to_all x1, blocking collectives: 20.9 us -> 20 us  [local(): gathered = lax.all_to_all(offs, 'neuron', 0, 0)]
    unnamed x16 -> x14, local copies, waits for them, and re-layouts: 3.91 us -> 3.22 us
  transfers between devices with their start and end apart: 2 -> 3, of which waited for: 2 -> 3; matrix products, arithmetic and copies ran while one was open for 0% -> 0% of each run, Pallas kernels for 6% -> 5%
where the time goes in v4:
time: 82.4 us; the launch traced here: 82.1 us
  waiting for transfers between devices  25 us (30%)
  starting transfers between devices  21.2 us (26%)
  blocking collectives  20 us (24%)
  Pallas kernels  11.7 us (14%)
  local copies, waits for them, and re-layouts  3.22 us (4%)
    ppermute x3, waiting for transfers between devices, send(): return lax.ppermute(value, 'neuron', pairs)  25 us
    ppermute x3, starting transfers between devices, send(): return lax.ppermute(value, 'neuron', pairs)  21.2 us
    all_to_all x1, blocking collectives, local(): gathered = lax.all_to_all(offs, 'neuron', 0, 0)  20 us
    pallas_call x1, Pallas kernels, first(): pl.pallas_call(functools.partial(first_kernel, total_blocks), out_shape=(...  5.9 us
    pallas_call x1, Pallas kernels, second(): pl.pallas_call(second_kernel, out_shape=(pltpu.VMEM((rows, width), jnp.fl...  3.71 us
    unnamed x14, local copies, waits for them, and re-layouts  3.22 us
  transfers between devices with their start and end apart: 3, of which 3 were waited for; matrix products, arithmetic and copies ran while one was open for 0% of the time, Pallas kernels for 5%

profile of v4, /device:TPU:24, one launch (start us, length us, event | category | flops | bytes accessed | tf_op | source)
XLA Modules:
  0.0 82.1 jit_solution(3959295809396159120)
XLA Ops:
  0.6 0.0 copy-start.6
  0.6 0.0 copy-start.5
  0.7 0.0 copy-start.4
  0.7 0.0 copy-start.3
  0.7 0.0 copy-start.2
  0.7 5.9 %first.1 = (f32[216,1024]{1,0:T(8,128)S(1)}, f32[216,1024]{1,0:T(8,128)S(1)}, bf16[216,1024]{1,0:T(8,128)(2,1)}, s32[16,128]{1,0:T(8,128)S(1)}) custom-call(s32[1]{0:T(128)} %bitcast.base_ref, s32[24]{0:T(128)} %labels_hbm.1, s32[16,32]{1,0:T(8,128)} %cols_hbm.1, bf16[10,24,1024]{2,1,0:T(8,128)(2,1)} %bitcast.12, bf16[16,64,2048]{2,1,0:T(8,128)(2,1)} %weights_hbm.3), custom_call_target="tpu_custom_call" | custom-call | flops 905969664 | bytes 6291456 | tf_op jit(solution)/shard_map/first/pallas_call | solution.py:179
  6.6 0.1 broadcast_select_fusion
  6.7 15.3 %collective-permute-start.2 = (f32[216,1024]{1,0:T(8,128)S(1)}, f32[216,1024]{1,0:T(8,128)S(1)}, u32[]{:S(2)}, u32[]{:S(2)}) collective-permute-start(f32[216,1024]{1,0:T(8,128)S(1)} %broadcast_select_fusion), channel_id=1, source_target_pairs={{0,31},{8,7},{16,15},{24,23},{7,8},{15,16},{23,24},{31,0},{32,63},... | collective-permute-start | bytes 2654216 | tf_op jit(solution)/shard_map/ppermute | solution.py:19
  22.1 1.3 %collective-permute-start = (f32[216,1024]{1,0:T(8,128)S(1)}, f32[216,1024]{1,0:T(8,128)S(1)}, u32[]{:S(2)}, u32[]{:S(2)}) collective-permute-start(f32[216,1024]{1,0:T(8,128)S(1)} %get-tuple-element.15), channel_id=1, source_target_pairs={{1,0},{2,1},{3,2},{4,3},{5,4},{6,5},{7,6},{9,8},{10,9},{11,10},{12... | collective-permute-start | bytes 2654216 | tf_op jit(solution)/shard_map/ppermute | solution.py:19
  23.4 4.6 %collective-permute-start.1 = (f32[216,1024]{1,0:T(8,128)S(1)}, f32[216,1024]{1,0:T(8,128)S(1)}, u32[]{:S(2)}, u32[]{:S(2)}) collective-permute-start(f32[216,1024]{1,0:T(8,128)S(1)} %get-tuple-element.16), channel_id=1, source_target_pairs={{0,1},{1,2},{2,3},{3,4},{4,5},{5,6},{6,7},{8,9},{9,10},{10,11},{11... | collective-permute-start | bytes 2654216 | tf_op jit(solution)/shard_map/ppermute | solution.py:19
  28.0 0.0 copy-done.6
  28.0 0.0 copy-done.5
  28.0 0.0 copy-done.4
  28.0 0.0 copy-done.3
  28.0 0.0 copy-done.2
  28.0 0.0 copy-start
  28.1 2.2 %copy-done = bf16[16,64,2048]{2,1,0:T(8,128)(2,1)S(1)} copy-done((bf16[16,64,2048]{2,1,0:T(8,128)(2,1)S(1)}, bf16[16,64,2048]{2,1,0:T(8,128)(2,1)}, u32[]{:S(2)}) %copy-start) | copy-done | bytes 4194328
  30.2 0.0 copy-start.1
  30.2 1.0 %copy-done.1 = bf16[216,1024]{1,0:T(8,128)(2,1)S(1)} copy-done((bf16[216,1024]{1,0:T(8,128)(2,1)S(1)}, bf16[216,1024]{1,0:T(8,128)(2,1)}, u32[]{:S(2)}) %copy-start.1) | copy-done | bytes 442392
  31.3 3.7 %second.1 = (f32[216,1024]{1,0:T(8,128)S(1)}, f32[216,128]{1,0:T(8,128)S(1)}, f32[3,1024]{1,0:T(4,128)S(1)}) custom-call(s32[16]{0:T(128)S(1)} %copy-done.5, s32[16,128]{1,0:T(8,128)S(1)} %get-tuple-element.11.codes_vmem, f32[1,1024]{1,0:T(1,128)S(1)} %bitcast.8, f32[1,1024]{1,0:T(1,128)S(1)} %bitcast.9, f32[1,1024]{1,0:T(1,128)S(1)} %bitcast.10, ...), custom_call_target="tpu_custom_call" | custom-call | flops 452984832 | bytes 6291456 | tf_op jit(solution)/shard_map/second/pallas_call | solution.py:258
  35.0 7.6 %collective-permute-done.2.closing_ref = f32[216,1024]{1,0:T(8,128)S(1)} collective-permute-done((f32[216,1024]{1,0:T(8,128)S(1)}, f32[216,1024]{1,0:T(8,128)S(1)}, u32[]{:S(2)}, u32[]{:S(2)}) %collective-permute-start.2) | collective-permute-done | bytes 884768 | tf_op jit(solution)/shard_map/ppermute | solution.py:19
  42.6 16.0 %collective-permute-done.higher_ref = f32[216,1024]{1,0:T(8,128)S(1)} collective-permute-done((f32[216,1024]{1,0:T(8,128)S(1)}, f32[216,1024]{1,0:T(8,128)S(1)}, u32[]{:S(2)}, u32[]{:S(2)}) %collective-permute-start) | collective-permute-done | bytes 884768 | tf_op jit(solution)/shard_map/ppermute | solution.py:19
  58.6 1.4 %collective-permute-done.1.lower_ref = f32[216,1024]{1,0:T(8,128)S(1)} collective-permute-done((f32[216,1024]{1,0:T(8,128)S(1)}, f32[216,1024]{1,0:T(8,128)S(1)}, u32[]{:S(2)}, u32[]{:S(2)}) %collective-permute-start.1) | collective-permute-done | bytes 884768 | tf_op jit(solution)/shard_map/ppermute | solution.py:19
  60.0 0.5 sums.1
  60.5 20.0 %all_to_all.5.gathered_ref = f32[32,1,216]{2,1,0:T(1,128)S(1)} all-to-all(f32[32,1,216]{2,1,0:T(1,128)S(1)} %sums.1), channel_id=1, replica_groups=mesh['spec'=16,'neuron'=32] {'neuron'}, dimensions={0} | all-to-all | bytes 55296 | tf_op jit(solution)/shard_map/all_to_all | solution.py:421
  80.5 1.6 %last.1 = (bf16[9,24,1024]{2,1,0:T(8,128)(2,1)}, f32[9,24]{1,0:T(8,128)}) custom-call(f32[3,1024]{1,0:T(4,128)S(1)} %get-tuple-element.13.slopes_ref, f32[216,1024]{1,0:T(8,128)S(1)} %get-tuple-element.14.centre_ref, f32[216,1024]{1,0:T(8,128)S(1)} %collective-permute-done.higher_ref, f32[216,1024]{1,0:T(8,128)S(1)} %collective-permute-done.1.lower_ref, ...), custom_call_target="tpu_custom_call" | custom-call | tf_op jit(solution)/shard_map/last/pallas_call | solution.py:359
  (1 shorter events, 0.0 us)
Async XLA Ops:
  0.6 27.4 %copy-start.6 = (bf16[1024]{0:T(1024)(128)(2,1)S(1)}, bf16[1024]{0:T(1024)(128)(2,1)}, u32[]{:S(2)}) copy-start(bf16[1024]{0:T(1024)(128)(2,1)} %param.13) | copy-start | bytes 6148
  0.6 27.4 %copy-start.5 = (s32[16]{0:T(128)S(1)}, s32[16]{0:T(128)}, u32[]{:S(2)}) copy-start(s32[16]{0:T(128)} %flags_ref.1) | copy-start | bytes 196
  0.7 27.4 %copy-start.4 = (f32[1024]{0:T(1024)S(1)}, f32[1024]{0:T(1024)}, u32[]{:S(2)}) copy-start(f32[1024]{0:T(1024)} %param.16) | copy-start | bytes 12292
  0.7 27.4 %copy-start.3 = (f32[1024]{0:T(1024)S(1)}, f32[1024]{0:T(1024)}, u32[]{:S(2)}) copy-start(f32[1024]{0:T(1024)} %param.15) | copy-start | bytes 12292
  0.7 27.4 %copy-start.2 = (f32[1024]{0:T(1024)S(1)}, f32[1024]{0:T(1024)}, u32[]{:S(2)}) copy-start(f32[1024]{0:T(1024)} %param.14) | copy-start | bytes 12292
  6.7 35.9 %collective-permute-start.2 = (f32[216,1024]{1,0:T(8,128)S(1)}, f32[216,1024]{1,0:T(8,128)S(1)}, u32[]{:S(2)}, u32[]{:S(2)}) collective-permute-start(f32[216,1024]{1,0:T(8,128)S(1)} %broadcast_select_fusion), channel_id=1, source_target_pairs={{0,31},{8,7},{16,15},{24,23},{7,8},{15,16},{23,24},{31,0},{32,63},... | collective-permute-start | bytes 2654216 | tf_op jit(solution)/shard_map/ppermute | solution.py:19
  22.1 36.5 %collective-permute-start = (f32[216,1024]{1,0:T(8,128)S(1)}, f32[216,1024]{1,0:T(8,128)S(1)}, u32[]{:S(2)}, u32[]{:S(2)}) collective-permute-start(f32[216,1024]{1,0:T(8,128)S(1)} %get-tuple-element.15), channel_id=1, source_target_pairs={{1,0},{2,1},{3,2},{4,3},{5,4},{6,5},{7,6},{9,8},{10,9},{11,10},{12... | collective-permute-start | bytes 2654216 | tf_op jit(solution)/shard_map/ppermute | solution.py:19
  23.4 36.6 %collective-permute-start.1 = (f32[216,1024]{1,0:T(8,128)S(1)}, f32[216,1024]{1,0:T(8,128)S(1)}, u32[]{:S(2)}, u32[]{:S(2)}) collective-permute-start(f32[216,1024]{1,0:T(8,128)S(1)} %get-tuple-element.16), channel_id=1, source_target_pairs={{0,1},{1,2},{2,3},{3,4},{4,5},{5,6},{6,7},{8,9},{9,10},{10,11},{11... | collective-permute-start | bytes 2654216 | tf_op jit(solution)/shard_map/ppermute | solution.py:19
  28.0 2.2 %copy-start = (bf16[16,64,2048]{2,1,0:T(8,128)(2,1)S(1)}, bf16[16,64,2048]{2,1,0:T(8,128)(2,1)}, u32[]{:S(2)}) copy-start(bf16[16,64,2048]{2,1,0:T(8,128)(2,1)} %weights_hbm.3) | copy-start | bytes 12582916
  30.2 1.0 %copy-start.1 = (bf16[216,1024]{1,0:T(8,128)(2,1)S(1)}, bf16[216,1024]{1,0:T(8,128)(2,1)}, u32[]{:S(2)}) copy-start(bf16[216,1024]{1,0:T(8,128)(2,1)} %get-tuple-element.12.margin_hbm) | copy-start | bytes 1327108

commit v5 on v4

--- a/solution.py
+++ b/solution.py
@@ -84,7 +84,9 @@
         out[:, at] = product if c == 0 else out[:, at] + product
 
 
-def place_and_multiply(tiles_ref, spread_ref, codes_smem, codes_copy, margin_ref, copies, parts, outs):
+def place_and_multiply(
+    tiles_ref, spread_ref, codes_smem, codes_copy, margin_ref, copies, parts, outs, prepare
+):
     blocksize = tiles_ref.shape[0]
     block_rows = len(copies)
     packed = (tiles_ref.shape[1] - LANES) // (2 * block_rows)
@@ -95,14 +97,15 @@
         rows = range(c * per_chunk, (c + 1) * per_chunk)
         for r in rows:
             copies[r].wait()
-        if c > 0:
-            multiply(margin_ref, spread_ref, c - 1, outs)
         for r in rows:
             turn(tiles_ref, r, packed, blocksize)
         if c == 0:
+            prepare()
             codes_copy.wait()
         for i, r in enumerate(rows):
             place(tiles_ref, spread_ref, codes_smem, c, i, r, parts, width)
+        if c > 0:
+            multiply(margin_ref, spread_ref, c - 1, outs)
     multiply(margin_ref, spread_ref, CHUNKS - 1, outs)
 
 
@@ -149,23 +152,26 @@
     )
     codes_copy = pltpu.make_async_copy(codes_ref, codes_smem, small_sems.at[3])
     codes_copy.start()
-    labels_copy.wait()
-    row = lax.broadcasted_iota(jnp.int32, (samples, width), 0)
-    labels = jnp.zeros((samples, width), jnp.int32)
-    for s in range(samples):
-        labels = jnp.where(row == s, labels_ref[s], labels)
-    scores_copy.wait()
-    scores = [scores_ref[c].astype(jnp.float32) for c in range(classes)]
-    top = scores[0]
-    for c in range(1, classes):
-        top = jnp.where(labels == c, scores[c], top)
-    for j in range(classes - 1):
-        rest = jnp.where(labels > j, scores[j], scores[j + 1])
-        margin_ref[pl.ds(j * samples, samples), :] = (top - rest).astype(jnp.bfloat16)
     margin_copy = pltpu.make_async_copy(margin_ref, margin_hbm, small_sems.at[4])
-    margin_copy.start()
+
+    def prepare():
+        labels_copy.wait()
+        row = lax.broadcasted_iota(jnp.int32, (samples, width), 0)
+        labels = jnp.zeros((samples, width), jnp.int32)
+        for s in range(samples):
+            labels = jnp.where(row == s, labels_ref[s], labels)
+        scores_copy.wait()
+        scores = [scores_ref[c].astype(jnp.float32) for c in range(classes)]
+        top = scores[0]
+        for c in range(1, classes):
+            top = jnp.where(labels == c, scores[c], top)
+        for j in range(classes - 1):
+            rest = jnp.where(labels > j, scores[j], scores[j + 1])
+            margin_ref[pl.ds(j * samples, samples), :] = (top - rest).astype(jnp.bfloat16)
+        margin_copy.start()
+
     place_and_multiply(
-        tiles_ref, spread_ref, codes_smem, codes_copy, margin_ref, copies, (0, 2), (down_ref, up_ref)
+        tiles_ref, spread_ref, codes_smem, codes_copy, margin_ref, copies, (0, 2), (down_ref, up_ref), prepare
     )
     margin_copy.wait()
 
@@ -247,7 +253,7 @@
     slopes_ref[1:2] = up_slope
     slopes_ref[2:3] = jnp.maximum(lower, 0.0) - up_slope * lower
     place_and_multiply(
-        tiles_ref, spread_ref, codes_smem, codes_copy, margin_ref, copies, (1,), (centre_ref,)
+        tiles_ref, spread_ref, codes_smem, codes_copy, margin_ref, copies, (1,), (centre_ref,), lambda: None
     )
 
 
@@ -326,14 +332,22 @@
     closing_ref,
     gathered_ref,
     coef_hbm,
+    out_hbm,
+    coef_ref,
     out_ref,
-    coef_ref,
     coef_sems,
+    out_sem,
 ):
     specs, samples, _ = coef_ref.shape
+    total = gathered_ref[0]
+    for d in range(1, gathered_ref.shape[0]):
+        total = total + gathered_ref[d]
+    for j in range(specs):
+        out_ref[j : j + 1, :] = total[:, j * samples : (j + 1) * samples]
+    copies = [pltpu.make_async_copy(out_ref, out_hbm, out_sem)]
+    copies[0].start()
     low_slope = slopes_ref[0:1]
     up_slope = slopes_ref[1:2]
-    copies = []
     for j in range(specs):
         at = slice(j * samples, (j + 1) * samples)
         propagated = centre_ref[at] + higher_ref[at] + lower_ref[at] + closing_ref[at]
@@ -342,11 +356,6 @@
         coef_ref[j] = (low_slope * positive + up_slope * negative).astype(jnp.bfloat16)
         copies.append(pltpu.make_async_copy(coef_ref.at[j], coef_hbm.at[j], coef_sems.at[j]))
         copies[-1].start()
-    total = gathered_ref[0]
-    for d in range(1, gathered_ref.shape[0]):
-        total = total + gathered_ref[d]
-    for j in range(specs):
-        out_ref[j : j + 1, :] = total[:, j * samples : (j + 1) * samples]
     for copy in copies:
         copy.wait()
 
@@ -363,10 +372,12 @@
             jax.ShapeDtypeStruct((specs, samples), jnp.float32),
         ),
         in_specs=[vmem] * 6,
-        out_specs=(hbm, vmem),
+        out_specs=(hbm, hbm),
         scratch_shapes=[
             pltpu.VMEM((specs, samples, width), jnp.bfloat16),
+            pltpu.VMEM((specs, samples), jnp.float32),
             pltpu.SemaphoreType.DMA((specs,)),
+            pltpu.SemaphoreType.DMA,
         ],
         compiler_params=pltpu.CompilerParams(vmem_limit_bytes=16 << 20),
         name="last",

time: 82.4 us -> 81.5 us (0.989)
  Pallas kernels: 11.7 us -> 10.8 us
where the time goes in v5:
time: 81.5 us; the launch traced here: 81.2 us
  waiting for transfers between devices  25.1 us (31%)
  starting transfers between devices  21.2 us (26%)
  blocking collectives  20 us (25%)
  Pallas kernels  10.8 us (13%)
  local copies, waits for them, and re-layouts  3.22 us (4%)
    ppermute x3, waiting for transfers between devices, send(): return lax.ppermute(value, 'neuron', pairs)  25.1 us
    ppermute x3, starting transfers between devices, send(): return lax.ppermute(value, 'neuron', pairs)  21.2 us
    all_to_all x1, blocking collectives, local(): gathered = lax.all_to_all(offs, 'neuron', 0, 0)  20 us
    pallas_call x1, Pallas kernels, first(): pl.pallas_call(functools.partial(first_kernel, total_blocks), out_shape=(...  5.6 us
    pallas_call x1, Pallas kernels, second(): pl.pallas_call(second_kernel, out_shape=(pltpu.VMEM((rows, width), jnp.fl...  3.7 us
    unnamed x14, local copies, waits for them, and re-layouts  3.22 us
  transfers between devices with their start and end apart: 3, of which 3 were waited for; matrix products, arithmetic and copies ran while one was open for 0% of the time, Pallas kernels for 5%

profile of v5, /device:TPU:24, one launch (start us, length us, event | category | flops | bytes accessed | tf_op | source)
XLA Modules:
  0.0 81.2 jit_solution(9368119880342188196)
XLA Ops:
  0.6 0.0 copy-start.6
  0.6 0.0 copy-start.5
  0.7 0.0 copy-start.4
  0.7 0.0 copy-start.3
  0.7 0.0 copy-start.2
  0.7 5.6 %first.1 = (f32[216,1024]{1,0:T(8,128)S(1)}, f32[216,1024]{1,0:T(8,128)S(1)}, bf16[216,1024]{1,0:T(8,128)(2,1)}, s32[16,128]{1,0:T(8,128)S(1)}) custom-call(s32[1]{0:T(128)} %bitcast.base_ref, s32[24]{0:T(128)} %labels_hbm.1, s32[16,32]{1,0:T(8,128)} %cols_hbm.1, bf16[10,24,1024]{2,1,0:T(8,128)(2,1)} %bitcast.12, bf16[16,64,2048]{2,1,0:T(8,128)(2,1)} %weights_hbm.3), custom_call_target="tpu_custom_call" | custom-call | flops 905969664 | bytes 6291456 | tf_op jit(solution)/shard_map/first/pallas_call | solution.py:185
  6.3 0.1 broadcast_select_fusion
  6.4 15.3 %collective-permute-start.2 = (f32[216,1024]{1,0:T(8,128)S(1)}, f32[216,1024]{1,0:T(8,128)S(1)}, u32[]{:S(2)}, u32[]{:S(2)}) collective-permute-start(f32[216,1024]{1,0:T(8,128)S(1)} %broadcast_select_fusion), channel_id=1, source_target_pairs={{0,31},{8,7},{16,15},{24,23},{7,8},{15,16},{23,24},{31,0},{32,63},... | collective-permute-start | bytes 2654216 | tf_op jit(solution)/shard_map/ppermute | solution.py:19
  21.8 1.3 %collective-permute-start = (f32[216,1024]{1,0:T(8,128)S(1)}, f32[216,1024]{1,0:T(8,128)S(1)}, u32[]{:S(2)}, u32[]{:S(2)}) collective-permute-start(f32[216,1024]{1,0:T(8,128)S(1)} %get-tuple-element.15), channel_id=1, source_target_pairs={{1,0},{2,1},{3,2},{4,3},{5,4},{6,5},{7,6},{9,8},{10,9},{11,10},{12... | collective-permute-start | bytes 2654216 | tf_op jit(solution)/shard_map/ppermute | solution.py:19
  23.1 4.6 %collective-permute-start.1 = (f32[216,1024]{1,0:T(8,128)S(1)}, f32[216,1024]{1,0:T(8,128)S(1)}, u32[]{:S(2)}, u32[]{:S(2)}) collective-permute-start(f32[216,1024]{1,0:T(8,128)S(1)} %get-tuple-element.16), channel_id=1, source_target_pairs={{0,1},{1,2},{2,3},{3,4},{4,5},{5,6},{6,7},{8,9},{9,10},{10,11},{11... | collective-permute-start | bytes 2654216 | tf_op jit(solution)/shard_map/ppermute | solution.py:19
  27.7 0.0 copy-done.6
  27.7 0.0 copy-done.5
  27.7 0.0 copy-done.4
  27.7 0.0 copy-done.3
  27.7 0.0 copy-done.2
  27.7 0.0 copy-start
  27.8 2.2 %copy-done = bf16[16,64,2048]{2,1,0:T(8,128)(2,1)S(1)} copy-done((bf16[16,64,2048]{2,1,0:T(8,128)(2,1)S(1)}, bf16[16,64,2048]{2,1,0:T(8,128)(2,1)}, u32[]{:S(2)}) %copy-start) | copy-done | bytes 4194328
  29.9 0.0 copy-start.1
  29.9 1.0 %copy-done.1 = bf16[216,1024]{1,0:T(8,128)(2,1)S(1)} copy-done((bf16[216,1024]{1,0:T(8,128)(2,1)S(1)}, bf16[216,1024]{1,0:T(8,128)(2,1)}, u32[]{:S(2)}) %copy-start.1) | copy-done | bytes 442392
  31.0 3.7 %second.1 = (f32[216,1024]{1,0:T(8,128)S(1)}, f32[216,128]{1,0:T(8,128)S(1)}, f32[3,1024]{1,0:T(4,128)S(1)}) custom-call(s32[16]{0:T(128)S(1)} %copy-done.5, s32[16,128]{1,0:T(8,128)S(1)} %get-tuple-element.11.codes_vmem, f32[1,1024]{1,0:T(1,128)S(1)} %bitcast.8, f32[1,1024]{1,0:T(1,128)S(1)} %bitcast.9, f32[1,1024]{1,0:T(1,128)S(1)} %bitcast.10, ...), custom_call_target="tpu_custom_call" | custom-call | flops 452984832 | bytes 6291456 | tf_op jit(solution)/shard_map/second/pallas_call | solution.py:264
  34.7 7.7 %collective-permute-done.2.closing_ref = f32[216,1024]{1,0:T(8,128)S(1)} collective-permute-done((f32[216,1024]{1,0:T(8,128)S(1)}, f32[216,1024]{1,0:T(8,128)S(1)}, u32[]{:S(2)}, u32[]{:S(2)}) %collective-permute-start.2) | collective-permute-done | bytes 884768 | tf_op jit(solution)/shard_map/ppermute | solution.py:19
  42.3 16.0 %collective-permute-done.higher_ref = f32[216,1024]{1,0:T(8,128)S(1)} collective-permute-done((f32[216,1024]{1,0:T(8,128)S(1)}, f32[216,1024]{1,0:T(8,128)S(1)}, u32[]{:S(2)}, u32[]{:S(2)}) %collective-permute-start) | collective-permute-done | bytes 884768 | tf_op jit(solution)/shard_map/ppermute | solution.py:19
  58.3 1.4 %collective-permute-done.1.lower_ref = f32[216,1024]{1,0:T(8,128)S(1)} collective-permute-done((f32[216,1024]{1,0:T(8,128)S(1)}, f32[216,1024]{1,0:T(8,128)S(1)}, u32[]{:S(2)}, u32[]{:S(2)}) %collective-permute-start.1) | collective-permute-done | bytes 884768 | tf_op jit(solution)/shard_map/ppermute | solution.py:19
  59.7 0.5 sums.1
  60.2 20.0 %all_to_all.5.gathered_ref = f32[32,1,216]{2,1,0:T(1,128)S(1)} all-to-all(f32[32,1,216]{2,1,0:T(1,128)S(1)} %sums.1), channel_id=1, replica_groups=mesh['spec'=16,'neuron'=32] {'neuron'}, dimensions={0} | all-to-all | bytes 55296 | tf_op jit(solution)/shard_map/all_to_all | solution.py:432
  80.1 1.0 %last.1 = (bf16[9,24,1024]{2,1,0:T(8,128)(2,1)}, f32[9,24]{1,0:T(8,128)}) custom-call(f32[3,1024]{1,0:T(4,128)S(1)} %get-tuple-element.13.slopes_ref, f32[216,1024]{1,0:T(8,128)S(1)} %get-tuple-element.14.centre_ref, f32[216,1024]{1,0:T(8,128)S(1)} %collective-permute-done.higher_ref, f32[216,1024]{1,0:T(8,128)S(1)} %collective-permute-done.1.lower_ref, ...), custom_call_target="tpu_custom_call" | custom-call | tf_op jit(solution)/shard_map/last/pallas_call | solution.py:368
  (1 shorter events, 0.0 us)
Async XLA Ops:
  0.6 27.1 %copy-start.6 = (bf16[1024]{0:T(1024)(128)(2,1)S(1)}, bf16[1024]{0:T(1024)(128)(2,1)}, u32[]{:S(2)}) copy-start(bf16[1024]{0:T(1024)(128)(2,1)} %param.13) | copy-start | bytes 6148
  0.6 27.1 %copy-start.5 = (s32[16]{0:T(128)S(1)}, s32[16]{0:T(128)}, u32[]{:S(2)}) copy-start(s32[16]{0:T(128)} %flags_ref.1) | copy-start | bytes 196
  0.7 27.1 %copy-start.4 = (f32[1024]{0:T(1024)S(1)}, f32[1024]{0:T(1024)}, u32[]{:S(2)}) copy-start(f32[1024]{0:T(1024)} %param.16) | copy-start | bytes 12292
  0.7 27.1 %copy-start.3 = (f32[1024]{0:T(1024)S(1)}, f32[1024]{0:T(1024)}, u32[]{:S(2)}) copy-start(f32[1024]{0:T(1024)} %param.15) | copy-start | bytes 12292
  0.7 27.1 %copy-start.2 = (f32[1024]{0:T(1024)S(1)}, f32[1024]{0:T(1024)}, u32[]{:S(2)}) copy-start(f32[1024]{0:T(1024)} %param.14) | copy-start | bytes 12292
  6.4 35.9 %collective-permute-start.2 = (f32[216,1024]{1,0:T(8,128)S(1)}, f32[216,1024]{1,0:T(8,128)S(1)}, u32[]{:S(2)}, u32[]{:S(2)}) collective-permute-start(f32[216,1024]{1,0:T(8,128)S(1)} %broadcast_select_fusion), channel_id=1, source_target_pairs={{0,31},{8,7},{16,15},{24,23},{7,8},{15,16},{23,24},{31,0},{32,63},... | collective-permute-start | bytes 2654216 | tf_op jit(solution)/shard_map/ppermute | solution.py:19
  21.8 36.5 %collective-permute-start = (f32[216,1024]{1,0:T(8,128)S(1)}, f32[216,1024]{1,0:T(8,128)S(1)}, u32[]{:S(2)}, u32[]{:S(2)}) collective-permute-start(f32[216,1024]{1,0:T(8,128)S(1)} %get-tuple-element.15), channel_id=1, source_target_pairs={{1,0},{2,1},{3,2},{4,3},{5,4},{6,5},{7,6},{9,8},{10,9},{11,10},{12... | collective-permute-start | bytes 2654216 | tf_op jit(solution)/shard_map/ppermute | solution.py:19
  23.1 36.6 %collective-permute-start.1 = (f32[216,1024]{1,0:T(8,128)S(1)}, f32[216,1024]{1,0:T(8,128)S(1)}, u32[]{:S(2)}, u32[]{:S(2)}) collective-permute-start(f32[216,1024]{1,0:T(8,128)S(1)} %get-tuple-element.16), channel_id=1, source_target_pairs={{0,1},{1,2},{2,3},{3,4},{4,5},{5,6},{6,7},{8,9},{9,10},{10,11},{11... | collective-permute-start | bytes 2654216 | tf_op jit(solution)/shard_map/ppermute | solution.py:19
  27.7 2.2 %copy-start = (bf16[16,64,2048]{2,1,0:T(8,128)(2,1)S(1)}, bf16[16,64,2048]{2,1,0:T(8,128)(2,1)}, u32[]{:S(2)}) copy-start(bf16[16,64,2048]{2,1,0:T(8,128)(2,1)} %weights_hbm.3) | copy-start | bytes 12582916
  29.9 1.0 %copy-start.1 = (bf16[216,1024]{1,0:T(8,128)(2,1)S(1)}, bf16[216,1024]{1,0:T(8,128)(2,1)}, u32[]{:S(2)}) copy-start(bf16[216,1024]{1,0:T(8,128)(2,1)} %get-tuple-element.12.margin_hbm) | copy-start | bytes 1327108

commit v6 on v5

--- a/solution.py
+++ b/solution.py
@@ -117,7 +117,7 @@
     ]
 
 
-def first_kernel(
+def outgoing(
     total_blocks,
     base_ref,
     labels_hbm,
@@ -174,6 +174,92 @@
         tiles_ref, spread_ref, codes_smem, codes_copy, margin_ref, copies, (0, 2), (down_ref, up_ref), prepare
     )
     margin_copy.wait()
+
+
+def place_in_run(base_ref, weights_hbm):
+    per_dev = weights_hbm.shape[0]
+    return lax.rem(lax.div(base_ref[0] + per_dev, jnp.int32(per_dev)), jnp.int32(RUN))
+
+
+def first_kernel(total_blocks, base_ref, *refs):
+    @pl.when(place_in_run(base_ref, refs[3]) != RUN - 1)
+    def _():
+        outgoing(total_blocks, base_ref, *refs)
+
+
+def late_kernel(
+    total_blocks,
+    base_ref,
+    labels_hbm,
+    cols_hbm,
+    scores_hbm,
+    weights_hbm,
+    early_down_ref,
+    early_margin_hbm,
+    early_codes_ref,
+    down_ref,
+    margin_hbm,
+    codes_ref,
+    outer_ref,
+    *scratch,
+):
+    del early_margin_hbm, early_codes_ref
+    index = place_in_run(base_ref, weights_hbm)
+
+    @pl.when(index == RUN - 1)
+    def _():
+        outgoing(
+            total_blocks,
+            base_ref,
+            labels_hbm,
+            cols_hbm,
+            scores_hbm,
+            weights_hbm,
+            down_ref,
+            outer_ref,
+            margin_hbm,
+            codes_ref,
+            *scratch,
+        )
+
+    @pl.when(index == 0)
+    def _():
+        outer_ref[...] = early_down_ref[...]
+
+
+def late(total_blocks, base, labels, cols, scores, weights, down, margin, codes):
+    rows, width = down.shape
+    samples = labels.shape[0]
+    block_rows = weights.shape[0]
+    hbm = pl.BlockSpec(memory_space=pltpu.HBM)
+    vmem = pl.BlockSpec(memory_space=pltpu.VMEM)
+    return pl.pallas_call(
+        functools.partial(late_kernel, total_blocks),
+        out_shape=(
+            pltpu.VMEM((rows, width), jnp.float32),
+            jax.ShapeDtypeStruct((rows, width), jnp.bfloat16),
+            pltpu.VMEM((block_rows, LANES), jnp.int32),
+            pltpu.VMEM((rows, width), jnp.float32),
+        ),
+        in_specs=[pl.BlockSpec(memory_space=pltpu.SMEM), hbm, hbm, hbm, hbm, vmem, hbm, vmem],
+        out_specs=(vmem, hbm, vmem, vmem),
+        input_output_aliases={5: 0, 6: 1, 7: 2},
+        scratch_shapes=[
+            pltpu.SMEM((samples,), jnp.int32),
+            pltpu.VMEM(cols.shape, jnp.int32),
+            pltpu.VMEM(scores.shape, jnp.bfloat16),
+            pltpu.VMEM((rows, width), jnp.bfloat16),
+            *tile_scratch(weights, 2, width),
+            pltpu.SMEM((block_rows, LANES), jnp.int32),
+            pltpu.SemaphoreType.DMA((5,)),
+            pltpu.SemaphoreType.DMA((block_rows,)),
+        ],
+        compiler_params=pltpu.CompilerParams(vmem_limit_bytes=59 << 20),
+        cost_estimate=pl.CostEstimate(
+            flops=4 * rows * width * width, bytes_accessed=6 << 20, transcendentals=0
+        ),
+        name="late",
+    )(base, labels, cols, scores, weights, down, margin, codes)
 
 
 def first(total_blocks, base, labels, cols, scores, weights):
@@ -400,19 +486,18 @@
     devices = lax.axis_size("neuron")
     position = lax.axis_index("neuron")
     base = ((position - 1) * per_dev).astype(jnp.int32).reshape(1)
+    scores = jnp.transpose(class_scores, (1, 0, 2))
+    total_blocks = devices * per_dev
     down, up, margin, codes = first(
-        devices * per_dev,
-        base,
-        true_class,
-        col_blocks,
-        jnp.transpose(class_scores, (1, 0, 2)),
-        weight_blocks,
+        total_blocks, base, true_class, col_blocks, scores, weight_blocks
     )
     starts = range(0, devices, RUN)
     ends = range(RUN - 1, devices, RUN)
+    lower = send(up, [(i, i + 1) for i in range(devices) if i not in ends])
+    down, margin, codes, outer = late(
+        total_blocks, base, true_class, col_blocks, scores, weight_blocks, down, margin, codes
+    )
     higher = send(down, [(i, i - 1) for i in range(devices) if i not in starts])
-    lower = send(up, [(i, i + 1) for i in range(devices) if i not in ends])
-    outer = jnp.where(position % RUN == 0, down, up)
     closing = send(
         outer,
         [(i, (i - 1) % devices) for i in starts] + [(i, (i + 1) % devices) for i in ends],

time: 81.5 us -> 82 us (level)
  waiting for transfers between devices: 25.1 us -> 29.3 us
  starting transfers between devices: 21.2 us -> 18.7 us
  blocking collectives: 20 us -> 18.7 us
    ppermute x3, waiting for transfers between devices: 25.1 us -> 29.3 us  [send(): return lax.ppermute(value, 'neuron', pairs)]
    ppermute x3, starting transfers between devices: 21.2 us -> 18.7 us  [send(): return lax.ppermute(value, 'neuron', pairs)]
    all_to_all x1, blocking collectives: 20 us -> 18.7 us  [local(): gathered = lax.all_to_all(offs, 'neuron', 0, 0)]
  transfers between devices with their start and end apart: 3 -> 3, of which waited for: 3 -> 2; matrix products, arithmetic and copies ran while one was open for 0% -> 0% of each run, Pallas kernels for 5% -> 5%
where the time goes in v6:
time: 82 us; the launch traced here: 81.7 us
  waiting for transfers between devices  29.3 us (36%)
  starting transfers between devices  18.7 us (23%)
  blocking collectives  18.7 us (23%)
  Pallas kernels  11.1 us (14%)
  local copies, waits for them, and re-layouts  3.23 us (4%)
    ppermute x3, waiting for transfers between devices, send(): return lax.ppermute(value, 'neuron', pairs)  29.3 us
    ppermute x3, starting transfers between devices, send(): return lax.ppermute(value, 'neuron', pairs)  18.7 us
    all_to_all x1, blocking collectives, local(): gathered = lax.all_to_all(offs, 'neuron', 0, 0)  18.7 us
    pallas_call x1, Pallas kernels, first(): pl.pallas_call(functools.partial(first_kernel, total_blocks), out_shape=(...  5.6 us
    pallas_call x1, Pallas kernels, second(): pl.pallas_call(second_kernel, out_shape=(pltpu.VMEM((rows, width), jnp.fl...  3.7 us
    unnamed x14, local copies, waits for them, and re-layouts  3.23 us
  transfers between devices with their start and end apart: 3, of which 2 were waited for; matrix products, arithmetic and copies ran while one was open for 0% of the time, Pallas kernels for 5%

profile of v6, /device:TPU:24, one launch (start us, length us, event | category | flops | bytes accessed | tf_op | source)
XLA Modules:
  0.0 81.7 jit_solution(11932314441731162556)
XLA Ops:
  0.6 5.6 %first.1 = (f32[216,1024]{1,0:T(8,128)S(1)}, f32[216,1024]{1,0:T(8,128)S(1)}, bf16[216,1024]{1,0:T(8,128)(2,1)}, s32[16,128]{1,0:T(8,128)S(1)}) custom-call(s32[1]{0:T(128)} %bitcast.base_ref, s32[24]{0:T(128)} %labels_hbm.1, s32[16,32]{1,0:T(8,128)} %cols_hbm.1, bf16[10,24,1024]{2,1,0:T(8,128)(2,1)} %bitcast.12, bf16[16,64,2048]{2,1,0:T(8,128)(2,1)} %weights_hbm.3), custom_call_target="tpu_custom_call" | custom-call | flops 905969664 | bytes 6291456 | tf_op jit(solution)/shard_map/first/pallas_call | solution.py:271
  6.2 0.0 copy-start.6
  6.2 0.0 copy-start.2
  6.3 0.0 copy-start.3
  6.3 0.0 copy-start.4
  6.3 0.0 copy-start.5
  6.3 0.3 late.1
  6.6 1.3 %collective-permute-start = (f32[216,1024]{1,0:T(8,128)S(1)}, f32[216,1024]{1,0:T(8,128)S(1)}, u32[]{:S(2)}, u32[]{:S(2)}) collective-permute-start(f32[216,1024]{1,0:T(8,128)S(1)} %get-tuple-element.22), channel_id=1, source_target_pairs={{1,0},{2,1},{3,2},{4,3},{5,4},{6,5},{7,6},{9,8},{10,9},{11,10},{12... | collective-permute-start | bytes 2654216 | tf_op jit(solution)/shard_map/ppermute | solution.py:19
  7.9 16.1 %collective-permute-start.2 = (f32[216,1024]{1,0:T(8,128)S(1)}, f32[216,1024]{1,0:T(8,128)S(1)}, u32[]{:S(2)}, u32[]{:S(2)}) collective-permute-start(f32[216,1024]{1,0:T(8,128)S(1)} %get-tuple-element.24), channel_id=1, source_target_pairs={{0,31},{8,7},{16,15},{24,23},{7,8},{15,16},{23,24},{31,0},{32,63},... | collective-permute-start | bytes 2654216 | tf_op jit(solution)/shard_map/ppermute | solution.py:19
  24.0 1.3 %collective-permute-start.1 = (f32[216,1024]{1,0:T(8,128)S(1)}, f32[216,1024]{1,0:T(8,128)S(1)}, u32[]{:S(2)}, u32[]{:S(2)}) collective-permute-start(f32[216,1024]{1,0:T(8,128)S(1)} %get-tuple-element.23), channel_id=1, source_target_pairs={{0,1},{1,2},{2,3},{3,4},{4,5},{5,6},{6,7},{8,9},{9,10},{10,11},{11... | collective-permute-start | bytes 2654216 | tf_op jit(solution)/shard_map/ppermute | solution.py:19
  25.3 0.0 copy-done.6
  25.3 0.0 copy-done.2
  25.3 0.0 copy-done.3
  25.4 0.0 copy-done.4
  25.4 0.0 copy-done.5
  25.4 0.0 copy-start
  25.4 2.2 %copy-done = bf16[16,64,2048]{2,1,0:T(8,128)(2,1)S(1)} copy-done((bf16[16,64,2048]{2,1,0:T(8,128)(2,1)S(1)}, bf16[16,64,2048]{2,1,0:T(8,128)(2,1)}, u32[]{:S(2)}) %copy-start) | copy-done | bytes 4194328
  27.6 0.0 copy-start.1
  27.6 1.0 %copy-done.1 = bf16[216,1024]{1,0:T(8,128)(2,1)S(1)} copy-done((bf16[216,1024]{1,0:T(8,128)(2,1)S(1)}, bf16[216,1024]{1,0:T(8,128)(2,1)}, u32[]{:S(2)}) %copy-start.1) | copy-done | bytes 442392
  28.6 3.7 %second.1 = (f32[216,1024]{1,0:T(8,128)S(1)}, f32[216,128]{1,0:T(8,128)S(1)}, f32[3,1024]{1,0:T(4,128)S(1)}) custom-call(s32[16]{0:T(128)S(1)} %copy-done.5, s32[16,128]{1,0:T(8,128)S(1)} %get-tuple-element.18.codes_vmem, f32[1,1024]{1,0:T(1,128)S(1)} %bitcast.8, f32[1,1024]{1,0:T(1,128)S(1)} %bitcast.9, f32[1,1024]{1,0:T(1,128)S(1)} %bitcast.10, ...), custom_call_target="tpu_custom_call" | custom-call | flops 452984832 | bytes 6291456 | tf_op jit(solution)/shard_map/second/pallas_call | solution.py:350
  32.3 0.0 collective-permute-done.higher_ref
  32.3 28.0 %collective-permute-done.2.closing_ref = f32[216,1024]{1,0:T(8,128)S(1)} collective-permute-done((f32[216,1024]{1,0:T(8,128)S(1)}, f32[216,1024]{1,0:T(8,128)S(1)}, u32[]{:S(2)}, u32[]{:S(2)}) %collective-permute-start.2) | collective-permute-done | bytes 884768 | tf_op jit(solution)/shard_map/ppermute | solution.py:19
  60.3 1.3 %collective-permute-done.1.lower_ref = f32[216,1024]{1,0:T(8,128)S(1)} collective-permute-done((f32[216,1024]{1,0:T(8,128)S(1)}, f32[216,1024]{1,0:T(8,128)S(1)}, u32[]{:S(2)}, u32[]{:S(2)}) %collective-permute-start.1) | collective-permute-done | bytes 884768 | tf_op jit(solution)/shard_map/ppermute | solution.py:19
  61.6 0.5 sums.1
  62.0 18.7 %all_to_all.5.gathered_ref = f32[32,1,216]{2,1,0:T(1,128)S(1)} all-to-all(f32[32,1,216]{2,1,0:T(1,128)S(1)} %sums.1), channel_id=1, replica_groups=mesh['spec'=16,'neuron'=32] {'neuron'}, dimensions={0} | all-to-all | bytes 55296 | tf_op jit(solution)/shard_map/all_to_all | solution.py:517
  80.7 1.0 %last.1 = (bf16[9,24,1024]{2,1,0:T(8,128)(2,1)}, f32[9,24]{1,0:T(8,128)}) custom-call(f32[3,1024]{1,0:T(4,128)S(1)} %get-tuple-element.20.slopes_ref, f32[216,1024]{1,0:T(8,128)S(1)} %get-tuple-element.21.centre_ref, f32[216,1024]{1,0:T(8,128)S(1)} %collective-permute-done.higher_ref, f32[216,1024]{1,0:T(8,128)S(1)} %collective-permute-done.1.lower_ref, ...), custom_call_target="tpu_custom_call" | custom-call | tf_op jit(solution)/shard_map/last/pallas_call | solution.py:454
  (1 shorter events, 0.0 us)
Async XLA Ops:
  6.2 19.1 %copy-start.6 = (bf16[1024]{0:T(1024)(128)(2,1)S(1)}, bf16[1024]{0:T(1024)(128)(2,1)}, u32[]{:S(2)}) copy-start(bf16[1024]{0:T(1024)(128)(2,1)} %param.13) | copy-start | bytes 6148
  6.2 19.1 %copy-start.2 = (f32[1024]{0:T(1024)S(1)}, f32[1024]{0:T(1024)}, u32[]{:S(2)}) copy-start(f32[1024]{0:T(1024)} %param.14) | copy-start | bytes 12292
  6.3 19.1 %copy-start.3 = (f32[1024]{0:T(1024)S(1)}, f32[1024]{0:T(1024)}, u32[]{:S(2)}) copy-start(f32[1024]{0:T(1024)} %param.15) | copy-start | bytes 12292
  6.3 19.1 %copy-start.4 = (f32[1024]{0:T(1024)S(1)}, f32[1024]{0:T(1024)}, u32[]{:S(2)}) copy-start(f32[1024]{0:T(1024)} %param.16) | copy-start | bytes 12292
  6.3 19.1 %copy-start.5 = (s32[16]{0:T(128)S(1)}, s32[16]{0:T(128)}, u32[]{:S(2)}) copy-start(s32[16]{0:T(128)} %flags_ref.1) | copy-start | bytes 196
  6.6 25.7 %collective-permute-start = (f32[216,1024]{1,0:T(8,128)S(1)}, f32[216,1024]{1,0:T(8,128)S(1)}, u32[]{:S(2)}, u32[]{:S(2)}) collective-permute-start(f32[216,1024]{1,0:T(8,128)S(1)} %get-tuple-element.22), channel_id=1, source_target_pairs={{1,0},{2,1},{3,2},{4,3},{5,4},{6,5},{7,6},{9,8},{10,9},{11,10},{12... | collective-permute-start | bytes 2654216 | tf_op jit(solution)/shard_map/ppermute | solution.py:19
  7.9 52.4 %collective-permute-start.2 = (f32[216,1024]{1,0:T(8,128)S(1)}, f32[216,1024]{1,0:T(8,128)S(1)}, u32[]{:S(2)}, u32[]{:S(2)}) collective-permute-start(f32[216,1024]{1,0:T(8,128)S(1)} %get-tuple-element.24), channel_id=1, source_target_pairs={{0,31},{8,7},{16,15},{24,23},{7,8},{15,16},{23,24},{31,0},{32,63},... | collective-permute-start | bytes 2654216 | tf_op jit(solution)/shard_map/ppermute | solution.py:19
  24.0 37.6 %collective-permute-start.1 = (f32[216,1024]{1,0:T(8,128)S(1)}, f32[216,1024]{1,0:T(8,128)S(1)}, u32[]{:S(2)}, u32[]{:S(2)}) collective-permute-start(f32[216,1024]{1,0:T(8,128)S(1)} %get-tuple-element.23), channel_id=1, source_target_pairs={{0,1},{1,2},{2,3},{3,4},{4,5},{5,6},{6,7},{8,9},{9,10},{10,11},{11... | collective-permute-start | bytes 2654216 | tf_op jit(solution)/shard_map/ppermute | solution.py:19
  25.4 2.2 %copy-start = (bf16[16,64,2048]{2,1,0:T(8,128)(2,1)S(1)}, bf16[16,64,2048]{2,1,0:T(8,128)(2,1)}, u32[]{:S(2)}) copy-start(bf16[16,64,2048]{2,1,0:T(8,128)(2,1)} %weights_hbm.3) | copy-start | bytes 12582916
  27.6 1.0 %copy-start.1 = (bf16[216,1024]{1,0:T(8,128)(2,1)S(1)}, bf16[216,1024]{1,0:T(8,128)(2,1)}, u32[]{:S(2)}) copy-start(bf16[216,1024]{1,0:T(8,128)(2,1)} %get-tuple-element.19.margin_hbm) | copy-start | bytes 1327108
